TPU v7x, 256 devices: a whole 4x4x8 slice. The times are simulated.
256 devices in a mesh: mom: 64 (over z, x, core), tm: 4 (over y).
Axes of the slice: x: 4, y: 4, z: 8, core: 2. Of those that a mesh axis runs over, the one named last changes fastest.
Arguments:
- new_rows: float32 [4, 256, 16, 512], P(None, 'mom', None, 'tm'), may hold values from -9 to 9
- history: float32 [3, 2, 256, 512, 512], P(None, None, 'mom', 'tm'), may hold values from -0.25 to 0.25
- momentum_map: int32 [256], replicated, may hold values from 0 to 255, each once
- step_index: int32 [1], replicated, may hold values from 0 to 999
- history_len: int32 [1], replicated, may hold values from 256 to 512
Outputs:
- advanced_rows: float32 [4, 256, 16, 512], P(None, 'mom', None, 'tm')
Inputs may be any that keep to these rules, and one draw needn't show every extreme that they name: `momentum_map`: each number of 0 to 255 appears once.
All inputs are finite; a program needn't handle non-finite values.
Results may differ from a plain program's by a relative error of at most 0.0003.
Values sent between devices are 32-bit elements; how exact they have to be, the bound alone decides.
No kernel may reach another device: no remote copies, remote signals or barrier semaphores. Data moves between devices by JAX's collectives and lax.ppermute only.
A program may use at most 128 MiB of HBM per device.

v0:
```python
import jax
import jax.numpy as jnp
from jax import lax
from jax.sharding import Mesh
from jax.sharding import PartitionSpec as P

SIDE = 16
MOM = ("mom_0", "mom_1", "mom_2")


TIME_STEP = 0.2
COUPLING = 5.0
DRIVE_RATE = 0.3
PRECISE = lax.Precision.HIGHEST


def split_up(value, dim, length):
    lengths = value.shape
    parts = value.reshape(*lengths[:dim], length, lengths[dim] // length, *lengths[dim + 1 :])
    return jnp.moveaxis(parts, dim, 0)


def joined_along(parts, dim):
    lengths = list(parts.shape[1:])
    lengths[dim] *= parts.shape[0]
    return jnp.moveaxis(parts, 0, dim).reshape(lengths)


def turned_blocks(parts, axes, sequence):
    lengths = [lax.axis_size(a) for a in axes]
    parts = parts.reshape(*lengths, *parts.shape[1:])
    for k in sequence:
        parts = lax.all_to_all(parts, axes[k], split_axis=k, concat_axis=k, tiled=True)
    return parts.reshape(-1, *parts.shape[len(axes) :])


def exchange_by_chip(value, groups, sequence, split_dim, concat_dim):
    length = lax.axis_size(groups[0]) * lax.axis_size(groups[1])
    parts = split_up(value, split_dim, length)
    return joined_along(turned_blocks(parts, groups, sequence), concat_dim)


def sum_at_owner(value, axis, dim):
    length = lax.axis_size(axis)
    parts = lax.all_to_all(split_up(value, dim, length), axis, 0, 0, tiled=True)
    return jnp.sum(parts, axis=0)


def lattice_tables(momentum_map, side):
    mom_count = momentum_map.shape[0]
    sites = jnp.arange(mom_count, dtype=jnp.int32)
    mom_x = momentum_map // side
    mom_y = momentum_map % side
    site_x = sites // side
    site_y = sites % side
    winding = (site_x[:, None] * mom_x[None, :] + site_y[:, None] * mom_y[None, :]) % side
    phases = winding.astype(jnp.float32) * (2.0 * jnp.pi / side)
    return (jnp.cos(phases), jnp.sin(phases))


def band_energy(own_map, row_times, side):
    wave_x = (own_map // side).astype(jnp.float32) * (2.0 * jnp.pi / side)
    wave_y = (own_map % side).astype(jnp.float32) * (2.0 * jnp.pi / side)
    drift = DRIVE_RATE * row_times
    return -2.0 * (
        jnp.cos(wave_x[:, None] + drift[None, :]) + jnp.cos(wave_y[:, None] + drift[None, :])
    )


def to_sites(cosine_table, sine_table, lattice):
    mom_count = lattice.shape[1]
    paired = lattice.reshape(2, 2, mom_count, lattice.shape[2])
    parts_re = paired[:, 0]
    parts_im = paired[:, 1]

    def apply_table(table, values):
        return jnp.einsum("rk,wkc->wrc", table, values, precision=PRECISE)

    site_re = (apply_table(cosine_table, parts_re) - apply_table(sine_table, parts_im)) / mom_count
    site_im = (apply_table(cosine_table, parts_im) + apply_table(sine_table, parts_re)) / mom_count
    return jnp.stack([site_re, site_im], axis=1).reshape(4, cosine_table.shape[0], lattice.shape[2])


def from_sites(cosine_table, sine_table, lattice):
    paired = lattice.reshape(2, 2, lattice.shape[1], lattice.shape[2])
    parts_re = paired[:, 0]
    parts_im = paired[:, 1]

    def apply_table(table, values):
        return jnp.einsum("rk,wrc->wkc", table, values, precision=PRECISE)

    mom_re = apply_table(cosine_table, parts_re) + apply_table(sine_table, parts_im)
    mom_im = apply_table(cosine_table, parts_im) - apply_table(sine_table, parts_re)
    return jnp.stack([mom_re, mom_im], axis=1).reshape(4, cosine_table.shape[1], lattice.shape[2])


def bubble_term(left_re, left_im, right_re, right_im):
    square_re = left_re * left_re - left_im * left_im
    square_im = 2.0 * left_re * left_im
    factor = -COUPLING * COUPLING
    return (
        factor * (square_re * right_re + square_im * right_im),
        factor * (square_im * right_re - square_re * right_im),
    )


def bubble(lattice):
    ret_re, ret_im, less_re, less_im = (lattice[0], lattice[1], lattice[2], lattice[3])
    great_re = less_re + ret_re
    great_im = less_im + ret_im
    lesser_re, lesser_im = bubble_term(less_re, less_im, great_re, great_im)
    greater_re, greater_im = bubble_term(great_re, great_im, less_re, less_im)
    return jnp.stack([greater_re - lesser_re, greater_im - lesser_im, lesser_re, lesser_im])


def contract(energy_pair, stored_pair):
    product = jnp.einsum("akiu,bkus->abkis", energy_pair, stored_pair, precision=PRECISE)
    return (product[0, 0] - product[1, 1], product[0, 1] + product[1, 0])


def memory_integral(self_energy, history):
    ret_ret = contract(self_energy[0:2], history[0])
    ret_less = contract(self_energy[0:2], history[1])
    less_adv = contract(self_energy[2:4], history[2])
    return TIME_STEP * jnp.stack(
        [ret_ret[0], ret_ret[1], ret_less[0] + less_adv[0], ret_less[1] + less_adv[1]]
    )


def rotate(total):
    return jnp.stack([total[1], -total[0], total[3], -total[2]])


def body(new_rows, history, momentum_map, step_index, history_len):
    own_count = new_rows.shape[1]
    row_count = new_rows.shape[2]
    time_count = new_rows.shape[3]
    cosine_table, sine_table = lattice_tables(momentum_map, SIDE)
    mom_start = lax.axis_index(MOM) * own_count
    own_map = lax.dynamic_slice_in_dim(momentum_map, mom_start, own_count, 0)
    time_start = lax.axis_index("tm") * time_count
    positions = time_start + jnp.arange(time_count, dtype=jnp.int32)
    memory_mask = (positions < history_len[0]).astype(jnp.float32)
    first_times = step_index[0].astype(jnp.float32) + jnp.arange(row_count, dtype=jnp.int32).astype(
        jnp.float32
    )

    def slope(estimate, offset_steps):
        band = band_energy(own_map, (first_times + offset_steps) * TIME_STEP, SIDE)
        flattened = estimate.reshape(4, own_count, row_count * time_count)
        by_site = exchange_by_chip(flattened, (("mom_0", "mom_1"), "mom_2"), (1, 0), 2, 1)
        site_energy = from_sites(
            cosine_table, sine_table, bubble(to_sites(cosine_table, sine_table, by_site))
        )
        returned = lax.all_to_all(site_energy, MOM, split_axis=1, concat_axis=2, tiled=True)
        self_energy = returned.reshape(4, own_count, row_count, time_count)
        self_energy = self_energy * memory_mask
        partial_rows = memory_integral(self_energy, history)
        integral = sum_at_owner(partial_rows, "tm", 3)
        return rotate(band[None, :, :, None] * estimate + integral)

    current = new_rows
    for time_step in range(2):
        slope_now = slope(current, float(time_step))
        estimate = current + TIME_STEP * slope_now
        for corrector in range(2):
            estimate = current + 0.5 * TIME_STEP * (
                slope_now + slope(estimate, float(time_step + 1))
            )
        current = estimate
    return current


def solution(mesh):
    split = Mesh(mesh.devices.reshape(8, 4, 2, mesh.shape["tm"]), ("mom_0", "mom_1", "mom_2", "tm"))
    return jax.shard_map(
        body,
        mesh=split,
        in_specs=(P(None, MOM, None, "tm"), P(None, None, MOM, "tm", None), P(), P(), P()),
        out_specs=P(None, MOM, None, "tm"),
        check_vma=False,
    )
```

profile of v0, /device:TPU:1, one launch (start us, length us, event | category | flops | bytes accessed | tf_op | source)
XLA Modules:
  0.0 441.6 jit_solution(11826651672709812574)
XLA Ops:
  1.4 6.7 %all_to_all.180 = f32[2,1,16384]{2,1,0:T(1,128)S(1)} all-to-all(f32[2,1,16384]{2,1,0:T(1,128)S(1)} %reshape.1208), channel_id=1, replica_groups=mesh['mom_0'=8,'mom_1'=4,'mom_2'=2,'tm'=4] {'mom_2'}, dimensions={0} | all-to-all | bytes 262144 | tf_op jit(solution)/shard_map/all_to_all | solution.py:33
  11.4 9.6 %all-to-all-start.1 = ((f32[32,1,1024]{2,1,0:T(1,128)}), f32[32,1,1024]{2,1,0:T(1,128)S(1)}, u32[]{:S(2)}, u32[]{:S(2)}) async-start(f32[32,1,1024]{2,1,0:T(1,128)} %reshape.1210), calls=%async_computation.1 | async-start | bytes 262144 | tf_op jit(solution)/shard_map/all_to_all | solution.py:33
  21.7 5.7 %fusion.414 = (f32[1,2,4,128,512]{4,3,2,1,0:T(8,128)S(1)}, f32[1,2,4,128,512]{4,3,2,1,0:T(8,128)}, f32[1,2,4,128,512]{4,3,2,1,0:T(8,128)}) fusion(f32[3,2,4,128,512]{4,3,2,1,0:T(8,128)} %param.6), kind=kLoop, calls=%fused_computation.607 | loop fusion | bytes 12582912 | tf_op jit(solution)/shard_map/slice | solution.py:122
  45.2 8.6 %all-to-all-start.2 = ((f32[64,1,512]{2,1,0:T(1,128)}), f32[64,1,512]{2,1,0:T(1,128)S(1)}, u32[]{:S(2)}, u32[]{:S(2)}) async-start(f32[64,1,512]{2,1,0:T(1,128)} %reshape.1212), calls=%async_computation.2 | async-start | bytes 262144 | tf_op jit(solution)/shard_map/all_to_all | solution.py:155
  54.0 11.0 %all-to-all-done.2 = f32[64,1,512]{2,1,0:T(1,128)S(1)} async-done(((f32[64,1,512]{2,1,0:T(1,128)}), f32[64,1,512]{2,1,0:T(1,128)S(1)}, u32[]{:S(2)}, u32[]{:S(2)}) %all-to-all-start.2) | async-done | bytes 131104 | tf_op jit(solution)/shard_map/all_to_all | solution.py:155
  77.4 8.7 %all-to-all-done.3 = f32[4,4,4,16,128]{4,3,2,1,0:T(8,128)S(1)} async-done(((f32[4,4,4,16,128]{4,3,2,1,0:T(8,128)}), f32[4,4,4,16,128]{4,3,2,1,0:T(8,128)S(1)}, u32[]{:S(2)}, u32[]{:S(2)}) %all-to-all-start.3) | async-done | bytes 524320 | tf_op jit(solution)/shard_map/all_to_all | solution.py:45
  86.8 5.0 %all_to_all.181 = f32[2,1,16384]{2,1,0:T(1,128)S(1)} all-to-all(f32[2,1,16384]{2,1,0:T(1,128)S(1)} %reshape.1214), channel_id=1, replica_groups=mesh['mom_0'=8,'mom_1'=4,'mom_2'=2,'tm'=4] {'mom_2'}, dimensions={0} | all-to-all | bytes 262144 | tf_op jit(solution)/shard_map/all_to_all | solution.py:33
  94.0 12.6 %all_to_all.182 = f32[32,1,1024]{2,1,0:T(1,128)S(1)} all-to-all(f32[32,1,1024]{2,1,0:T(1,128)S(1)} %reshape.1216), channel_id=1, replica_groups=mesh['mom_0'=8,'mom_1'=4,'mom_2'=2,'tm'=4] {'mom_0','mom_1'}, dimensions={0} | all-to-all | bytes 262144 | tf_op jit(solution)/shard_map/all_to_all | solution.py:33
  120.8 16.8 %all_to_all.183 = f32[64,1,512]{2,1,0:T(1,128)S(1)} all-to-all(f32[64,1,512]{2,1,0:T(1,128)S(1)} %reshape.1218), channel_id=1, replica_groups=mesh['mom_0'=8,'mom_1'=4,'mom_2'=2,'tm'=4] {'mom_0','mom_1','mom_2'}, dimensions={0} | all-to-all | bytes 262144 | tf_op jit(solution)/shard_map/all_to_all | solution.py:155
  144.9 11.6 %all_to_all.184 = f32[4,4,4,16,128]{4,3,2,1,0:T(8,128)S(1)} all-to-all(f32[4,4,4,16,128]{4,3,2,1,0:T(8,128)S(1)} %fusion.69), channel_id=1, replica_groups=mesh['mom_0'=8,'mom_1'=4,'mom_2'=2,'tm'=4] {'tm'}, dimensions={0} | all-to-all | bytes 1048576 | tf_op jit(solution)/shard_map/all_to_all | solution.py:45
  157.2 4.7 %all_to_all.185 = f32[2,1,16384]{2,1,0:T(1,128)S(1)} all-to-all(f32[2,1,16384]{2,1,0:T(1,128)S(1)} %reshape.1220), channel_id=1, replica_groups=mesh['mom_0'=8,'mom_1'=4,'mom_2'=2,'tm'=4] {'mom_2'}, dimensions={0} | all-to-all | bytes 262144 | tf_op jit(solution)/shard_map/all_to_all | solution.py:33
  164.1 12.8 %all_to_all.186 = f32[32,1,1024]{2,1,0:T(1,128)S(1)} all-to-all(f32[32,1,1024]{2,1,0:T(1,128)S(1)} %reshape.1222), channel_id=1, replica_groups=mesh['mom_0'=8,'mom_1'=4,'mom_2'=2,'tm'=4] {'mom_0','mom_1'}, dimensions={0} | all-to-all | bytes 262144 | tf_op jit(solution)/shard_map/all_to_all | solution.py:33
  191.2 16.7 %all_to_all.187 = f32[64,1,512]{2,1,0:T(1,128)S(1)} all-to-all(f32[64,1,512]{2,1,0:T(1,128)S(1)} %reshape.1224), channel_id=1, replica_groups=mesh['mom_0'=8,'mom_1'=4,'mom_2'=2,'tm'=4] {'mom_0','mom_1','mom_2'}, dimensions={0} | all-to-all | bytes 262144 | tf_op jit(solution)/shard_map/all_to_all | solution.py:155
  215.2 11.6 %all_to_all.188 = f32[4,4,4,16,128]{4,3,2,1,0:T(8,128)S(1)} all-to-all(f32[4,4,4,16,128]{4,3,2,1,0:T(8,128)S(1)} %fusion.70), channel_id=1, replica_groups=mesh['mom_0'=8,'mom_1'=4,'mom_2'=2,'tm'=4] {'tm'}, dimensions={0} | all-to-all | bytes 1048576 | tf_op jit(solution)/shard_map/all_to_all | solution.py:45
  227.5 4.7 %all_to_all.189 = f32[2,1,16384]{2,1,0:T(1,128)S(1)} all-to-all(f32[2,1,16384]{2,1,0:T(1,128)S(1)} %reshape.1226), channel_id=1, replica_groups=mesh['mom_0'=8,'mom_1'=4,'mom_2'=2,'tm'=4] {'mom_2'}, dimensions={0} | all-to-all | bytes 262144 | tf_op jit(solution)/shard_map/all_to_all | solution.py:33
  234.4 12.6 %all_to_all.190 = f32[32,1,1024]{2,1,0:T(1,128)S(1)} all-to-all(f32[32,1,1024]{2,1,0:T(1,128)S(1)} %reshape.1228), channel_id=1, replica_groups=mesh['mom_0'=8,'mom_1'=4,'mom_2'=2,'tm'=4] {'mom_0','mom_1'}, dimensions={0} | all-to-all | bytes 262144 | tf_op jit(solution)/shard_map/all_to_all | solution.py:33
  261.3 16.9 %all_to_all.191 = f32[64,1,512]{2,1,0:T(1,128)S(1)} all-to-all(f32[64,1,512]{2,1,0:T(1,128)S(1)} %reshape.1230), channel_id=1, replica_groups=mesh['mom_0'=8,'mom_1'=4,'mom_2'=2,'tm'=4] {'mom_0','mom_1','mom_2'}, dimensions={0} | all-to-all | bytes 262144 | tf_op jit(solution)/shard_map/all_to_all | solution.py:155
  285.5 11.6 %all_to_all.192 = f32[4,4,4,16,128]{4,3,2,1,0:T(8,128)S(1)} all-to-all(f32[4,4,4,16,128]{4,3,2,1,0:T(8,128)S(1)} %fusion.71), channel_id=1, replica_groups=mesh['mom_0'=8,'mom_1'=4,'mom_2'=2,'tm'=4] {'tm'}, dimensions={0} | all-to-all | bytes 1048576 | tf_op jit(solution)/shard_map/all_to_all | solution.py:45
  305.3 12.6 %all_to_all.194 = f32[32,1,1024]{2,1,0:T(1,128)S(1)} all-to-all(f32[32,1,1024]{2,1,0:T(1,128)S(1)} %reshape.1234), channel_id=1, replica_groups=mesh['mom_0'=8,'mom_1'=4,'mom_2'=2,'tm'=4] {'mom_0','mom_1'}, dimensions={0} | all-to-all | bytes 262144 | tf_op jit(solution)/shard_map/all_to_all | solution.py:33
  332.2 16.8 %all_to_all.195 = f32[64,1,512]{2,1,0:T(1,128)S(1)} all-to-all(f32[64,1,512]{2,1,0:T(1,128)S(1)} %reshape.1236), channel_id=1, replica_groups=mesh['mom_0'=8,'mom_1'=4,'mom_2'=2,'tm'=4] {'mom_0','mom_1','mom_2'}, dimensions={0} | all-to-all | bytes 262144 | tf_op jit(solution)/shard_map/all_to_all | solution.py:155
  357.9 11.6 %all_to_all.196 = f32[4,4,4,16,128]{4,3,2,1,0:T(8,128)S(1)} all-to-all(f32[4,4,4,16,128]{4,3,2,1,0:T(8,128)S(1)} %fusion.72), channel_id=1, replica_groups=mesh['mom_0'=8,'mom_1'=4,'mom_2'=2,'tm'=4] {'tm'}, dimensions={0} | all-to-all | bytes 1048576 | tf_op jit(solution)/shard_map/all_to_all | solution.py:45
  377.7 12.8 %all_to_all.198 = f32[32,1,1024]{2,1,0:T(1,128)S(1)} all-to-all(f32[32,1,1024]{2,1,0:T(1,128)S(1)} %reshape.1240), channel_id=1, replica_groups=mesh['mom_0'=8,'mom_1'=4,'mom_2'=2,'tm'=4] {'mom_0','mom_1'}, dimensions={0} | all-to-all | bytes 262144 | tf_op jit(solution)/shard_map/all_to_all | solution.py:33
  404.8 16.7 %all_to_all.199 = f32[64,1,512]{2,1,0:T(1,128)S(1)} all-to-all(f32[64,1,512]{2,1,0:T(1,128)S(1)} %reshape.1242), channel_id=1, replica_groups=mesh['mom_0'=8,'mom_1'=4,'mom_2'=2,'tm'=4] {'mom_0','mom_1','mom_2'}, dimensions={0} | all-to-all | bytes 262144 | tf_op jit(solution)/shard_map/all_to_all | solution.py:155
  428.9 11.6 %all_to_all.200 = f32[4,4,4,16,128]{4,3,2,1,0:T(8,128)S(1)} all-to-all(f32[4,4,4,16,128]{4,3,2,1,0:T(8,128)S(1)} %fusion.73), channel_id=1, replica_groups=mesh['mom_0'=8,'mom_1'=4,'mom_2'=2,'tm'=4] {'tm'}, dimensions={0} | all-to-all | bytes 1048576 | tf_op jit(solution)/shard_map/all_to_all | solution.py:45
  (420 shorter events, 167.5 us)
Async XLA Ops:
  11.4 18.7 %all-to-all-start.1 = ((f32[32,1,1024]{2,1,0:T(1,128)}), f32[32,1,1024]{2,1,0:T(1,128)S(1)}, u32[]{:S(2)}, u32[]{:S(2)}) async-start(f32[32,1,1024]{2,1,0:T(1,128)} %reshape.1210), calls=%async_computation.1 | async-start | bytes 262144 | tf_op jit(solution)/shard_map/all_to_all | solution.py:33
  21.0 21.0 %copy-start.39 = (s32[256]{0:T(256)}, s32[256]{0:T(256)S(1)}, u32[]{:S(2)}) copy-start(s32[256]{0:T(256)S(1)} %and_select_fusion.3) | copy-start | bytes 3076
  21.7 6.4 %copy-start.27 = (s32[256]{0:T(256)S(1)}, s32[256]{0:T(256)}, u32[]{:S(2)}) copy-start(s32[256]{0:T(256)} %param.7) | copy-start | bytes 3076
  28.1 13.9 %copy-start.28 = (s32[256]{0:T(256)}, s32[256]{0:T(256)S(1)}, u32[]{:S(2)}) copy-start(s32[256]{0:T(256)S(1)} %get-tuple-element.100) | copy-start | bytes 3076
  28.1 13.9 %copy-start.33 = (s32[256]{0:T(256)}, s32[256]{0:T(256)S(1)}, u32[]{:S(2)}) copy-start(s32[256]{0:T(256)S(1)} %get-tuple-element.101) | copy-start | bytes 3076
  45.2 19.8 %all-to-all-start.2 = ((f32[64,1,512]{2,1,0:T(1,128)}), f32[64,1,512]{2,1,0:T(1,128)S(1)}, u32[]{:S(2)}, u32[]{:S(2)}) async-start(f32[64,1,512]{2,1,0:T(1,128)} %reshape.1212), calls=%async_computation.2 | async-start | bytes 262144 | tf_op jit(solution)/shard_map/all_to_all | solution.py:155
  72.1 14.1 %copy-start.6 = (f32[4,4,16,128]{3,2,1,0:T(8,128)S(1)}, f32[4,4,16,128]{3,2,1,0:T(8,128)}, u32[]{:S(2)}) copy-start(f32[4,4,16,128]{3,2,1,0:T(8,128)} %param.5) | copy-start | bytes 393220
  73.1 13.1 %all-to-all-start.3 = ((f32[4,4,4,16,128]{4,3,2,1,0:T(8,128)}), f32[4,4,4,16,128]{4,3,2,1,0:T(8,128)S(1)}, u32[]{:S(2)}, u32[]{:S(2)}) async-start(f32[4,4,4,16,128]{4,3,2,1,0:T(8,128)} %fusion.68), calls=%async_computation.3 | async-start | bytes 1048576 | tf_op jit(solution)/shard_map/all_to_all | solution.py:45
  106.6 4.0 copy-start.40
  176.9 4.0 copy-start.41
  304.8 15.1 %copy-start.32 = (s32[256]{0:T(256)S(1)}, s32[256]{0:T(256)}, u32[]{:S(2)}) copy-start(s32[256]{0:T(256)} %copy-done.28) | copy-start | bytes 3076
  317.9 4.0 copy-start.43
  356.7 12.8 %copy-start.8 = (f32[1,4,16,128]{3,2,1,0:T(8,128)S(1)}, f32[1,4,16,128]{3,2,1,0:T(8,128)}, u32[]{:S(2)}) copy-start(f32[1,4,16,128]{3,2,1,0:T(8,128)} %copy-done.7) | copy-start | bytes 98308
  356.7 12.8 %copy-start.11 = (f32[1,4,16,128]{3,2,1,0:T(8,128)S(1)}, f32[1,4,16,128]{3,2,1,0:T(8,128)}, u32[]{:S(2)}) copy-start(f32[1,4,16,128]{3,2,1,0:T(8,128)} %copy-done.10) | copy-start | bytes 98308
  356.7 12.8 %copy-start.14 = (f32[1,4,16,128]{3,2,1,0:T(8,128)S(1)}, f32[1,4,16,128]{3,2,1,0:T(8,128)}, u32[]{:S(2)}) copy-start(f32[1,4,16,128]{3,2,1,0:T(8,128)} %copy-done.13) | copy-start | bytes 98308
  356.7 12.8 %copy-start.17 = (f32[1,4,16,128]{3,2,1,0:T(8,128)S(1)}, f32[1,4,16,128]{3,2,1,0:T(8,128)}, u32[]{:S(2)}) copy-start(f32[1,4,16,128]{3,2,1,0:T(8,128)} %copy-done.16) | copy-start | bytes 98308
  428.6 12.0 %copy-start.9 = (f32[1,4,16,128]{3,2,1,0:T(8,128)S(1)}, f32[1,4,16,128]{3,2,1,0:T(8,128)}, u32[]{:S(2)}) copy-start(f32[1,4,16,128]{3,2,1,0:T(8,128)} %copy-done.7) | copy-start | bytes 98308
  428.6 12.0 %copy-start.12 = (f32[1,4,16,128]{3,2,1,0:T(8,128)S(1)}, f32[1,4,16,128]{3,2,1,0:T(8,128)}, u32[]{:S(2)}) copy-start(f32[1,4,16,128]{3,2,1,0:T(8,128)} %copy-done.10) | copy-start | bytes 98308
  428.6 12.0 %copy-start.15 = (f32[1,4,16,128]{3,2,1,0:T(8,128)S(1)}, f32[1,4,16,128]{3,2,1,0:T(8,128)}, u32[]{:S(2)}) copy-start(f32[1,4,16,128]{3,2,1,0:T(8,128)} %copy-done.13) | copy-start | bytes 98308
  428.6 12.0 %copy-start.18 = (f32[1,4,16,128]{3,2,1,0:T(8,128)S(1)}, f32[1,4,16,128]{3,2,1,0:T(8,128)}, u32[]{:S(2)}) copy-start(f32[1,4,16,128]{3,2,1,0:T(8,128)} %copy-done.16) | copy-start | bytes 98308
  428.6 12.0 %copy-start.20 = (f32[1,4,16,128]{3,2,1,0:T(8,128)S(1)}, f32[1,4,16,128]{3,2,1,0:T(8,128)}, u32[]{:S(2)}) copy-start(f32[1,4,16,128]{3,2,1,0:T(8,128)} %copy-done.19) | copy-start | bytes 98308
  428.7 12.0 %copy-start.22 = (f32[1,4,16,128]{3,2,1,0:T(8,128)S(1)}, f32[1,4,16,128]{3,2,1,0:T(8,128)}, u32[]{:S(2)}) copy-start(f32[1,4,16,128]{3,2,1,0:T(8,128)} %copy-done.21) | copy-start | bytes 98308
  428.7 12.0 %copy-start.24 = (f32[1,4,16,128]{3,2,1,0:T(8,128)S(1)}, f32[1,4,16,128]{3,2,1,0:T(8,128)}, u32[]{:S(2)}) copy-start(f32[1,4,16,128]{3,2,1,0:T(8,128)} %copy-done.23) | copy-start | bytes 98308
  428.7 12.0 %copy-start.26 = (f32[1,4,16,128]{3,2,1,0:T(8,128)S(1)}, f32[1,4,16,128]{3,2,1,0:T(8,128)}, u32[]{:S(2)}) copy-start(f32[1,4,16,128]{3,2,1,0:T(8,128)} %copy-done.25) | copy-start | bytes 98308
  (24 other events, 63.0 us)
where the time goes:
time: 445 us; the launch traced here: 442 us
  blocking collectives  236 us (53%)
  matrix products  101 us (23%)
  local copies, waits for them, and re-layouts  34.9 us (8%)
  starting transfers between devices  22.4 us (5%)
  waiting for transfers between devices  21.6 us (5%)
  other arithmetic  21.5 us (5%)
    all_to_all x11, blocking collectives, turned_blocks(): lax.all_to_all(parts, axes[k], split_axis=k, concat_axis=k, tiled=True)  93.9 us
    all_to_all x5, blocking collectives, slope(): lax.all_to_all(site_energy, MOM, split_axis=1, concat_axis=2, tiled=True)  83.9 us
    all_to_all x5, blocking collectives, sum_at_owner(): parts = lax.all_to_all(split_up(value, dim, length), axis, 0, 0, tiled=True)  58 us
    dot_general x24, matrix products, apply_table(): return jnp.einsum('rk,wrc->wkc', table, values, precision=PRECISE)  32.2 us
    dot_general x18, matrix products, contract(): jnp.einsum('akiu,bkus->abkis', energy_pair, stored_pair, precision=PRECISE)  32.1 us
    dot_general x20, matrix products, apply_table(): return jnp.einsum('rk,wkc->wrc', table, values, precision=PRECISE)  31.3 us
    unnamed x128, local copies, waits for them, and re-layouts  15.4 us
    all_to_all x1, waiting for transfers between devices, slope(): lax.all_to_all(site_energy, MOM, split_axis=1, concat_axis=2, tiled=True)  11 us
  transfers between devices with their start and end apart: 3, of which 3 were waited for; matrix products, arithmetic and copies ran while one was open for 1% of the time, Pallas kernels for 0%

commit v1 on v0

v1 whole, which is shorter than its diff:
```python
import functools

import jax
import jax.numpy as jnp
from jax import lax
from jax.experimental import pallas as pl
from jax.experimental.pallas import tpu as pltpu
from jax.sharding import PartitionSpec as P

SIDE = 16
TIME_STEP = 0.2
COUPLING = 5.0
DRIVE_RATE = 0.3
LANES = 128
GROUP = 32
F32 = jnp.float32
BF16 = jnp.bfloat16


def lane_group(shape):
    return lax.broadcasted_iota(jnp.int32, shape, len(shape) - 1) // GROUP


def swap_groups(blocks):
    group = lane_group(blocks[0].shape)
    outs = []
    for c in range(4):
        out = None
        for q in range(4):
            shift = (GROUP * (q - c)) % LANES
            piece = pltpu.roll(blocks[q], shift, 1) if shift else blocks[q]
            out = piece if out is None else jnp.where(group == q, piece, out)
        outs.append(out)
    return outs


def split_high_low(value):
    high = value.astype(BF16)
    low = (value - high.astype(F32)).astype(BF16)
    return high, low


def times_minus_i(value):
    even = lane_group(value.shape) % 2 == 0
    return jnp.where(even, pltpu.roll(value, LANES - GROUP, 1), -pltpu.roll(value, GROUP, 1))


def resident(kernel, out_shapes, in_spaces, name, scratch=(), limit=4 << 20):
    results = [pltpu.VMEM(o.shape, o.dtype) for o in out_shapes]
    call = pl.pallas_call(
        kernel,
        in_specs=[pl.BlockSpec(memory_space=space) for space in in_spaces],
        out_specs=[pl.BlockSpec(memory_space=pltpu.VMEM)] * len(results),
        out_shape=results,
        scratch_shapes=scratch,
        compiler_params=pltpu.CompilerParams(vmem_limit_bytes=limit),
        name=name,
    )

    def apply(*values):
        placed = [
            value if space is pltpu.SMEM else pltpu.with_memory_space_constraint(value, space)
            for value, space in zip(values, in_spaces, strict=True)
        ]
        return call(*placed)

    return apply


def pack_kernel(rows_ref, out_ref):
    row_count = rows_ref.shape[2]
    own = rows_ref.shape[1]
    for k in range(own):
        packed = swap_groups([rows_ref[c, k] for c in range(4)])
        for q in range(4):
            out_ref[pl.ds(q * own * row_count + k, row_count, stride=own), :] = packed[q]


def history_kernel(stored_ref, high_ref, low_ref, buffer_ref, arrived):
    kinds, parts, own, times, _ = stored_ref.shape
    slots = buffer_ref.shape[0]

    def fetch(n):
        slot = n % slots
        return pltpu.make_async_copy(stored_ref.at[n // parts, n % parts], buffer_ref.at[slot], arrived.at[slot])

    for n in range(slots):
        fetch(n).start()
    for n in range(kinds * parts):
        fetch(n).wait()
        for k in range(own):
            high, low = split_high_low(buffer_ref[n % slots, k])
            high_ref[k, n * times : (n + 1) * times, :] = high
            low_ref[k, n * times : (n + 1) * times, :] = low
        if n + slots < kinds * parts:
            fetch(n + slots).start()


def transform(table_ref, value, turned):
    value_high, value_low = split_high_low(value)
    turned_high, turned_low = split_high_low(turned)
    operand = jnp.concatenate(
        [
            jnp.concatenate([value_high, value_low], axis=1),
            jnp.concatenate([turned_high, turned_low], axis=1),
        ],
        axis=0,
    )
    depth = operand.shape[0]
    total = jnp.dot(table_ref[:, :depth], operand, preferred_element_type=F32)
    total = total + jnp.dot(table_ref[:, depth:], operand, preferred_element_type=F32)
    return total[:, :LANES] + total[:, LANES:]


def site_kernel(table_ref, rows_ref, out_ref):
    mom_count = rows_ref.shape[0]
    rows = rows_ref[...]
    group = lane_group(rows.shape)
    even = group % 2 == 0
    upper = group >= 2
    sites = transform(table_ref, rows, -times_minus_i(rows)) * (1.0 / mom_count)
    other = pltpu.roll(sites, 2 * GROUP, 1)
    great = sites + other
    less = jnp.where(upper, sites, other)
    great_turn = pltpu.roll(great, GROUP, 1)
    less_turn = pltpu.roll(less, GROUP, 1)
    pair = jnp.where(even, less * great + less_turn * great_turn, less * great_turn - less_turn * great)
    pair_turn = pltpu.roll(pair, GROUP, 1)
    lesser = jnp.where(even, less * pair - less_turn * pair_turn, less * pair_turn + less_turn * pair)
    greater = jnp.where(even, great * pair + great_turn * pair_turn, great * pair_turn - great_turn * pair)
    energy = (-COUPLING * COUPLING) * jnp.where(upper, lesser, greater - lesser)
    out_ref[...] = transform(table_ref, energy, times_minus_i(energy))


def integral_kernel(limits_ref, energy_ref, high_ref, low_ref, out_ref, split_ref):
    own = high_ref.shape[0]
    block = split_ref.shape[1]
    rows = block // own
    position = limits_ref[0] + lax.broadcasted_iota(jnp.int32, (block, LANES), 1)
    mask = (position < limits_ref[1]).astype(F32)
    parts = swap_groups([energy_ref[q * block : (q + 1) * block, :] for q in range(4)])
    for c in range(4):
        split_ref[c] = parts[c] * mask

    def left(k, pair):
        real = split_ref[2 * pair, pl.ds(k, rows, stride=own), :]
        imag = split_ref[2 * pair + 1, pl.ds(k, rows, stride=own), :]
        joined = jnp.concatenate(
            [jnp.concatenate([real, -imag], axis=1), jnp.concatenate([imag, real], axis=1)], axis=0
        )
        high, low = split_high_low(joined)
        return jnp.concatenate([high, low], axis=0)

    for k in range(own):
        retarded_left = left(k, 0)
        lesser_left = jnp.concatenate([retarded_left, left(k, 1)], axis=1)

        def product(lhs, start, stop):
            both = jnp.dot(lhs, high_ref[k, start:stop, :], preferred_element_type=F32)
            small = jnp.dot(lhs[: 2 * rows], low_ref[k, start:stop, :], preferred_element_type=F32)
            return TIME_STEP * (both[: 2 * rows] + both[2 * rows :] + small)

        retarded = product(retarded_left, 0, 2 * LANES)
        lesser = product(lesser_left, 2 * LANES, 6 * LANES)
        values = (retarded[:rows], retarded[rows:], lesser[:rows], lesser[rows:])
        for t in range(out_ref.shape[0]):
            for c, value in enumerate(values):
                out_ref[t, pl.ds(c * block + k, rows, stride=own), :] = value[:, t * LANES : (t + 1) * LANES]


def slope_of(parts_ref, state, band_ref):
    block = band_ref.shape[0]
    total = parts_ref[0]
    for t in range(1, parts_ref.shape[0]):
        total = total + parts_ref[t]
    packed = swap_groups([total[c * block : (c + 1) * block] for c in range(4)])
    band = band_ref[...]
    return jnp.concatenate(
        [times_minus_i(band * state[q * block : (q + 1) * block] + packed[q]) for q in range(4)], axis=0
    )


def predict_kernel(parts_ref, state_ref, band_ref, out_ref, base_ref):
    state = state_ref[...]
    slope = slope_of(parts_ref, state, band_ref)
    out_ref[...] = state + TIME_STEP * slope
    base_ref[...] = state + (0.5 * TIME_STEP) * slope


def correct_kernel(parts_ref, state_ref, band_ref, base_ref, out_ref):
    slope = slope_of(parts_ref, state_ref[...], band_ref)
    out_ref[...] = base_ref[...] + (0.5 * TIME_STEP) * slope


def last_kernel(parts_ref, state_ref, band_ref, base_ref, out_ref, split_ref):
    slope = slope_of(parts_ref, state_ref[...], band_ref)
    value = base_ref[...] + (0.5 * TIME_STEP) * slope
    block = band_ref.shape[0]
    parts = swap_groups([value[q * block : (q + 1) * block] for q in range(4)])
    own, rows = out_ref.shape[1], out_ref.shape[2]
    for c in range(4):
        split_ref[c] = parts[c]
        for k in range(own):
            out_ref[c, k] = split_ref[c, pl.ds(k, rows, stride=own), :]


def transform_tables(momentum_map):
    point_x = momentum_map // SIDE
    point_y = momentum_map % SIDE
    winding = (point_x[:, None] * point_x[None, :] + point_y[:, None] * point_y[None, :]) % SIDE
    phases = winding.astype(F32) * (2.0 * jnp.pi / SIDE)
    parts = []
    for table in (jnp.cos(phases), jnp.sin(phases)):
        high = lax.reduce_precision(table, 8, 7)
        parts.append((high.astype(BF16), (table - high).astype(BF16)))
    (cos_high, cos_low), (sin_high, sin_low) = parts
    return jnp.concatenate([cos_high, sin_high, cos_low, sin_low], axis=1)


def band_rows(own_map, first_times, offset):
    wave_x = (own_map // SIDE).astype(F32) * (2.0 * jnp.pi / SIDE)
    wave_y = (own_map % SIDE).astype(F32) * (2.0 * jnp.pi / SIDE)
    drift = DRIVE_RATE * ((first_times + offset) * TIME_STEP)
    band = -2.0 * (jnp.cos(wave_x[None, :] + drift[:, None]) + jnp.cos(wave_y[None, :] + drift[:, None]))
    return jnp.broadcast_to(band.reshape(-1, 1), (band.size, LANES))


def body(new_rows, history, momentum_map, step_index, history_len):
    own = new_rows.shape[1]
    row_count = new_rows.shape[2]
    time_count = new_rows.shape[3]
    hist = history.shape[4]
    block = own * row_count
    packed_shape = jax.ShapeDtypeStruct((4 * block, time_count), F32)

    table = transform_tables(momentum_map)
    own_map = lax.dynamic_slice_in_dim(momentum_map, lax.axis_index("mom") * own, own, 0)
    first_times = step_index[0].astype(F32) + jnp.arange(row_count, dtype=jnp.int32).astype(F32)
    bands = [band_rows(own_map, first_times, float(offset)) for offset in range(3)]
    limits = jnp.stack([lax.axis_index("tm") * time_count, history_len[0]])

    vmem = pltpu.VMEM
    pack = resident(pack_kernel, [packed_shape], [vmem], "pack")
    stored = 6 * time_count
    split_shape = jax.ShapeDtypeStruct((own, stored, hist), BF16)
    split_history = resident(
        history_kernel,
        [split_shape] * 2,
        [pltpu.HBM],
        "split_history",
        [vmem((3, *history.shape[2:]), F32), pltpu.SemaphoreType.DMA((3,))],
        5 << 20,
    )
    site = resident(site_kernel, [packed_shape], [vmem] * 2, "site")
    tm_size = lax.axis_size("tm")
    parts_shape = jax.ShapeDtypeStruct((tm_size, 4 * block, LANES), F32)
    integral = resident(
        integral_kernel, [parts_shape], [pltpu.SMEM] + [vmem] * 3, "integral", [vmem((4, block, LANES), F32)]
    )
    predict = resident(predict_kernel, [packed_shape] * 2, [vmem] * 3, "predict")
    correct = resident(correct_kernel, [packed_shape], [vmem] * 4, "correct")
    last = pl.pallas_call(
        last_kernel,
        out_shape=jax.ShapeDtypeStruct(new_rows.shape, F32),
        scratch_shapes=[pltpu.VMEM((4, block, LANES), F32)],
        name="last",
    )

    (state,) = pack(new_rows)
    high, low = split_history(history)

    def turned(value):
        return lax.all_to_all(value, "mom", 0, 0, tiled=True)

    def parts_of(arrived):
        (energy,) = site(table, arrived)
        (partial,) = integral(limits, turned(energy), high, low)
        return lax.all_to_all(partial, "tm", 0, 0, tiled=True)

    first = turned(state)
    first, table, high, low, limits, bands, state = lax.optimization_barrier(
        (first, table, high, low, limits, bands, state)
    )

    for time_step in range(2):
        arrived = first if time_step == 0 else turned(state)
        estimate, base = predict(parts_of(arrived), state, bands[time_step])
        (estimate,) = correct(parts_of(turned(estimate)), estimate, bands[time_step + 1], base)
        if time_step == 0:
            (state,) = correct(parts_of(turned(estimate)), estimate, bands[time_step + 1], base)
    return last(parts_of(turned(estimate)), estimate, bands[2], base)


def solution(mesh):
    return jax.shard_map(
        body,
        mesh=mesh,
        in_specs=(P(None, "mom", None, "tm"), P(None, None, "mom", "tm", None), P(), P(), P()),
        out_specs=P(None, "mom", None, "tm"),
        check_vma=False,
    )
```

time: 445 us -> 300 us (0.67)
  matrix products: 101 us -> 0 us
  local copies, waits for them, and re-layouts: 34.9 us -> 5.99 us
  Pallas kernels: 0 us -> 26.1 us
  waiting for transfers between devices: 21.6 us -> 0.01 us
  other arithmetic: 21.5 us -> 5.59 us
  blocking collectives: 236 us -> 247 us
  starting transfers between devices: 22.4 us -> 13 us
    dot_general x62 -> x0, matrix products: 95.6 us -> none  [the longest x24 32.2 us: apply_table(): return jnp.einsum('rk,wrc->wkc', table, values, precision=PRECISE)]
    pallas_call x0 -> x20, Pallas kernels: none -> 26.1 us  [the longest x19 23.8 us: apply(): return call(*placed)]
    all_to_all x3 -> x1, waiting for transfers between devices: 21.6 us -> 0.01 us  [turned(): return lax.all_to_all(value, 'mom', 0, 0, tiled=True)]
    all_to_all x18 -> x0, other arithmetic: 16.1 us -> none  [the longest x12 10.9 us: turned_blocks(): lax.all_to_all(parts, axes[k], split_axis=k, concat_axis=k, tiled=True)]
    all_to_all x21 -> x17, blocking collectives: 236 us -> 247 us  [the longest x11 175 us: turned(): return lax.all_to_all(value, 'mom', 0, 0, tiled=True)]
    unnamed x128 -> x18, local copies, waits for them, and re-layouts: 15.4 us -> 5.52 us
    all_to_all x3 -> x1, starting transfers between devices: 22.4 us -> 13 us  [turned(): return lax.all_to_all(value, 'mom', 0, 0, tiled=True)]
    slice x2 -> x0, local copies, waits for them, and re-layouts: 5.76 us -> none  [the longest x1 5.72 us: memory_integral(): ret_ret = contract(self_energy[0:2], history[0])]
  transfers between devices with their start and end apart: 3 -> 1, of which waited for: 3 -> 0; matrix products, arithmetic and copies ran while one was open for 1% -> 2% of each run, Pallas kernels for 0% -> 1%
where the time goes in v1:
time: 300 us; the launch traced here: 299 us
  blocking collectives  247 us (82%)
  Pallas kernels  26.1 us (9%)
  starting transfers between devices  13 us (4%)
  local copies, waits for them, and re-layouts  5.99 us (2%)
  other arithmetic  5.59 us (2%)
    all_to_all x11, blocking collectives, turned(): return lax.all_to_all(value, 'mom', 0, 0, tiled=True)  175 us
    all_to_all x6, blocking collectives, parts_of(): return lax.all_to_all(partial, 'tm', 0, 0, tiled=True)  71.3 us
    pallas_call x19, Pallas kernels, apply(): return call(*placed)  23.8 us
    all_to_all x1, starting transfers between devices, turned(): return lax.all_to_all(value, 'mom', 0, 0, tiled=True)  13 us
  transfers between devices with their start and end apart: 1, of which 0 were waited for; matrix products, arithmetic and copies ran while one was open for 2% of the time, Pallas kernels for 1%

profile of v1, /device:TPU:1, one launch (start us, length us, event | category | flops | bytes accessed | tf_op | source)
XLA Modules:
  0.0 298.8 jit_solution(9374237348444221912)
XLA Ops:
  1.7 13.0 %all-to-all-start = ((f32[64,4,128]{2,1,0:T(4,128)}), f32[64,4,128]{2,1,0:T(4,128)S(1)}, u32[]{:S(2)}, u32[]{:S(2)}) async-start(f32[64,4,128]{2,1,0:T(4,128)} %bitcast), calls=%async_computation | async-start | bytes 262144 | tf_op jit(solution)/shard_map/all_to_all | solution.py:273
  16.9 2.0 reduce-precision_convert_fusion.1
  20.0 3.5 %split_history.1 = (bf16[4,768,512]{2,1,0:T(8,128)(2,1)S(1)}, bf16[4,768,512]{2,1,0:T(8,128)(2,1)S(1)}) custom-call(f32[3,2,4,128,512]{4,3,2,1,0:T(8,128)} %stored_ref.1), custom_call_target="tpu_custom_call" | custom-call | tf_op jit(solution)/shard_map/split_history/pallas_call | solution.py:65
  25.2 1.8 pad_maximum_fusion.table_ref
  29.4 21.2 %all_to_all.163 = f32[64,4,128]{2,1,0:T(4,128)S(1)} all-to-all(f32[64,4,128]{2,1,0:T(4,128)S(1)} %bitcast.37), channel_id=1, replica_groups=mesh['mom'=64,'tm'=4] {'mom'}, dimensions={0} | all-to-all | bytes 262144 | tf_op jit(solution)/shard_map/all_to_all | solution.py:273
  50.7 1.9 copy-done.1
  54.4 12.6 %all_to_all.164.parts_ref = f32[4,256,128]{2,1,0:T(8,128)S(1)} all-to-all(f32[4,256,128]{2,1,0:T(8,128)S(1)} %integral.6), channel_id=1, replica_groups=mesh['mom'=64,'tm'=4] {'tm'}, dimensions={0} | all-to-all | bytes 1048576 | tf_op jit(solution)/shard_map/all_to_all | solution.py:278
  68.1 16.4 %all_to_all.165 = f32[64,4,128]{2,1,0:T(4,128)S(1)} all-to-all(f32[64,4,128]{2,1,0:T(4,128)S(1)} %bitcast.47), channel_id=1, replica_groups=mesh['mom'=64,'tm'=4] {'mom'}, dimensions={0} | all-to-all | bytes 262144 | tf_op jit(solution)/shard_map/all_to_all | solution.py:273
  85.6 14.9 %all_to_all.166 = f32[64,4,128]{2,1,0:T(4,128)S(1)} all-to-all(f32[64,4,128]{2,1,0:T(4,128)S(1)} %bitcast.38), channel_id=1, replica_groups=mesh['mom'=64,'tm'=4] {'mom'}, dimensions={0} | all-to-all | bytes 262144 | tf_op jit(solution)/shard_map/all_to_all | solution.py:273
  100.5 1.8 integral.7
  102.3 11.6 %all_to_all.167.parts_ref = f32[4,256,128]{2,1,0:T(8,128)S(1)} all-to-all(f32[4,256,128]{2,1,0:T(8,128)S(1)} %integral.7), channel_id=1, replica_groups=mesh['mom'=64,'tm'=4] {'tm'}, dimensions={0} | all-to-all | bytes 1048576 | tf_op jit(solution)/shard_map/all_to_all | solution.py:278
  114.2 15.8 %all_to_all.168 = f32[64,4,128]{2,1,0:T(4,128)S(1)} all-to-all(f32[64,4,128]{2,1,0:T(4,128)S(1)} %bitcast.28), channel_id=1, replica_groups=mesh['mom'=64,'tm'=4] {'mom'}, dimensions={0} | all-to-all | bytes 262144 | tf_op jit(solution)/shard_map/all_to_all | solution.py:273
  131.1 15.1 %all_to_all.169 = f32[64,4,128]{2,1,0:T(4,128)S(1)} all-to-all(f32[64,4,128]{2,1,0:T(4,128)S(1)} %bitcast.39), channel_id=1, replica_groups=mesh['mom'=64,'tm'=4] {'mom'}, dimensions={0} | all-to-all | bytes 262144 | tf_op jit(solution)/shard_map/all_to_all | solution.py:273
  148.0 11.6 %all_to_all.170.parts_ref = f32[4,256,128]{2,1,0:T(8,128)S(1)} all-to-all(f32[4,256,128]{2,1,0:T(8,128)S(1)} %integral.8), channel_id=1, replica_groups=mesh['mom'=64,'tm'=4] {'tm'}, dimensions={0} | all-to-all | bytes 1048576 | tf_op jit(solution)/shard_map/all_to_all | solution.py:278
  159.8 15.8 %all_to_all.171 = f32[64,4,128]{2,1,0:T(4,128)S(1)} all-to-all(f32[64,4,128]{2,1,0:T(4,128)S(1)} %bitcast.26), channel_id=1, replica_groups=mesh['mom'=64,'tm'=4] {'mom'}, dimensions={0} | all-to-all | bytes 262144 | tf_op jit(solution)/shard_map/all_to_all | solution.py:273
  176.7 14.9 %all_to_all.172 = f32[64,4,128]{2,1,0:T(4,128)S(1)} all-to-all(f32[64,4,128]{2,1,0:T(4,128)S(1)} %bitcast.40), channel_id=1, replica_groups=mesh['mom'=64,'tm'=4] {'mom'}, dimensions={0} | all-to-all | bytes 262144 | tf_op jit(solution)/shard_map/all_to_all | solution.py:273
  193.4 11.6 %all_to_all.173.parts_ref = f32[4,256,128]{2,1,0:T(8,128)S(1)} all-to-all(f32[4,256,128]{2,1,0:T(8,128)S(1)} %integral.9), channel_id=1, replica_groups=mesh['mom'=64,'tm'=4] {'tm'}, dimensions={0} | all-to-all | bytes 1048576 | tf_op jit(solution)/shard_map/all_to_all | solution.py:278
  205.3 15.8 %all_to_all.174 = f32[64,4,128]{2,1,0:T(4,128)S(1)} all-to-all(f32[64,4,128]{2,1,0:T(4,128)S(1)} %bitcast.48), channel_id=1, replica_groups=mesh['mom'=64,'tm'=4] {'mom'}, dimensions={0} | all-to-all | bytes 262144 | tf_op jit(solution)/shard_map/all_to_all | solution.py:273
  222.2 14.9 %all_to_all.175 = f32[64,4,128]{2,1,0:T(4,128)S(1)} all-to-all(f32[64,4,128]{2,1,0:T(4,128)S(1)} %bitcast.41), channel_id=1, replica_groups=mesh['mom'=64,'tm'=4] {'mom'}, dimensions={0} | all-to-all | bytes 262144 | tf_op jit(solution)/shard_map/all_to_all | solution.py:273
  238.9 11.6 %all_to_all.176.parts_ref = f32[4,256,128]{2,1,0:T(8,128)S(1)} all-to-all(f32[4,256,128]{2,1,0:T(8,128)S(1)} %integral.10), channel_id=1, replica_groups=mesh['mom'=64,'tm'=4] {'tm'}, dimensions={0} | all-to-all | bytes 1048576 | tf_op jit(solution)/shard_map/all_to_all | solution.py:278
  250.8 15.7 %all_to_all.177 = f32[64,4,128]{2,1,0:T(4,128)S(1)} all-to-all(f32[64,4,128]{2,1,0:T(4,128)S(1)} %bitcast.27), channel_id=1, replica_groups=mesh['mom'=64,'tm'=4] {'mom'}, dimensions={0} | all-to-all | bytes 262144 | tf_op jit(solution)/shard_map/all_to_all | solution.py:273
  267.6 14.9 %all_to_all.178 = f32[64,4,128]{2,1,0:T(4,128)S(1)} all-to-all(f32[64,4,128]{2,1,0:T(4,128)S(1)} %bitcast.36), channel_id=1, replica_groups=mesh['mom'=64,'tm'=4] {'mom'}, dimensions={0} | all-to-all | bytes 262144 | tf_op jit(solution)/shard_map/all_to_all | solution.py:273
  284.3 12.3 %all_to_all.179.parts_ref = f32[4,256,128]{2,1,0:T(8,128)} all-to-all(f32[4,256,128]{2,1,0:T(8,128)S(1)} %integral.11), channel_id=1, replica_groups=mesh['mom'=64,'tm'=4] {'tm'}, dimensions={0} | all-to-all | bytes 1048576 | tf_op jit(solution)/shard_map/all_to_all | solution.py:278
  296.6 2.2 last.1
  (48 shorter events, 24.4 us)
Async XLA Ops:
  0.0 0.9 copy-start.8
  1.7 25.3 %all-to-all-start = ((f32[64,4,128]{2,1,0:T(4,128)}), f32[64,4,128]{2,1,0:T(4,128)S(1)}, u32[]{:S(2)}, u32[]{:S(2)}) async-start(f32[64,4,128]{2,1,0:T(4,128)} %bitcast), calls=%async_computation | async-start | bytes 262144 | tf_op jit(solution)/shard_map/all_to_all | solution.py:273
  23.5 1.6 copy-start
  27.3 223.2 %copy-start.7 = (f32[64,128]{1,0:T(8,128)}, f32[64,128]{1,0:T(8,128)S(1)}, u32[]{:S(2)}) copy-start(f32[64,128]{1,0:T(8,128)S(1)} %broadcast_in_dim.8.band_ref) | copy-start | bytes 98308
  27.3 1.1 copy-start.3
  50.7 1.9 copy-start.1
  52.5 31.9 %copy-start.4 = (bf16[256,1024]{1,0:T(8,128)(2,1)S(1)}, bf16[256,1024]{1,0:T(8,128)(2,1)}, u32[]{:S(2)}) copy-start(bf16[256,1024]{1,0:T(8,128)(2,1)} %pad_maximum_fusion.table_ref) | copy-start | bytes 1572868
  52.6 48.0 %copy-start.2 = (bf16[4,768,512]{2,1,0:T(8,128)(2,1)S(1)}, bf16[4,768,512]{2,1,0:T(8,128)(2,1)}, u32[]{:S(2)}) copy-start(bf16[4,768,512]{2,1,0:T(8,128)(2,1)} %copy-done) | copy-start | bytes 9437188
  205.3 45.2 %copy-start.6 = (f32[256,128]{1,0:T(8,128)}, f32[256,128]{1,0:T(8,128)S(1)}, u32[]{:S(2)}) copy-start(f32[256,128]{1,0:T(8,128)S(1)} %get-tuple-element.34.base_ref) | copy-start | bytes 393220
  250.8 33.5 %copy-start.5 = (f32[256,128]{1,0:T(8,128)}, f32[256,128]{1,0:T(8,128)S(1)}, u32[]{:S(2)}) copy-start(f32[256,128]{1,0:T(8,128)S(1)} %correct.5.state_ref) | copy-start | bytes 393220

commit v2 on v1

--- a/solution.py
+++ b/solution.py
@@ -74,26 +74,6 @@
         packed = swap_groups([rows_ref[c, k] for c in range(4)])
         for q in range(4):
             out_ref[pl.ds(q * own * row_count + k, row_count, stride=own), :] = packed[q]
-
-
-def history_kernel(stored_ref, high_ref, low_ref, buffer_ref, arrived):
-    kinds, parts, own, times, _ = stored_ref.shape
-    slots = buffer_ref.shape[0]
-
-    def fetch(n):
-        slot = n % slots
-        return pltpu.make_async_copy(stored_ref.at[n // parts, n % parts], buffer_ref.at[slot], arrived.at[slot])
-
-    for n in range(slots):
-        fetch(n).start()
-    for n in range(kinds * parts):
-        fetch(n).wait()
-        for k in range(own):
-            high, low = split_high_low(buffer_ref[n % slots, k])
-            high_ref[k, n * times : (n + 1) * times, :] = high
-            low_ref[k, n * times : (n + 1) * times, :] = low
-        if n + slots < kinds * parts:
-            fetch(n + slots).start()
 
 
 def transform(table_ref, value, turned):
@@ -132,11 +112,13 @@
     out_ref[...] = transform(table_ref, energy, times_minus_i(energy))
 
 
-def integral_kernel(limits_ref, energy_ref, high_ref, low_ref, out_ref, split_ref):
-    own = high_ref.shape[0]
+def integral_into(limits_ref, energy_ref, parts_ref, out_refs, split_ref, prepare=None):
+    step_one = limits_ref[0] % 2 == 1
+    step_two = limits_ref[0] // 2 == 1
+    own = parts_ref.shape[1]
     block = split_ref.shape[1]
     rows = block // own
-    position = limits_ref[0] + lax.broadcasted_iota(jnp.int32, (block, LANES), 1)
+    position = limits_ref[0] * LANES + lax.broadcasted_iota(jnp.int32, (block, LANES), 1)
     mask = (position < limits_ref[1]).astype(F32)
     parts = swap_groups([energy_ref[q * block : (q + 1) * block, :] for q in range(4)])
     for c in range(4):
@@ -151,28 +133,60 @@
         high, low = split_high_low(joined)
         return jnp.concatenate([high, low], axis=0)
 
-    for k in range(own):
+    def product(k, lhs, start, stop):
+        both = jnp.dot(lhs, parts_ref[0, k, start:stop, :], preferred_element_type=F32)
+        small = jnp.dot(lhs[: 2 * rows], parts_ref[1, k, start:stop, :], preferred_element_type=F32)
+        return TIME_STEP * (both[: 2 * rows] + both[2 * rows :] + small)
+
+    def each(k, carry):
+        if prepare is not None:
+            prepare(k)
         retarded_left = left(k, 0)
         lesser_left = jnp.concatenate([retarded_left, left(k, 1)], axis=1)
-
-        def product(lhs, start, stop):
-            both = jnp.dot(lhs, high_ref[k, start:stop, :], preferred_element_type=F32)
-            small = jnp.dot(lhs[: 2 * rows], low_ref[k, start:stop, :], preferred_element_type=F32)
-            return TIME_STEP * (both[: 2 * rows] + both[2 * rows :] + small)
-
-        retarded = product(retarded_left, 0, 2 * LANES)
-        lesser = product(lesser_left, 2 * LANES, 6 * LANES)
+        retarded = product(k, retarded_left, 0, 2 * LANES)
+        lesser = product(k, lesser_left, 2 * LANES, 6 * LANES)
         values = (retarded[:rows], retarded[rows:], lesser[:rows], lesser[rows:])
-        for t in range(out_ref.shape[0]):
-            for c, value in enumerate(values):
-                out_ref[t, pl.ds(c * block + k, rows, stride=own), :] = value[:, t * LANES : (t + 1) * LANES]
-
-
-def slope_of(parts_ref, state, band_ref):
+        for c, value in enumerate(values):
+            pieces = [value[:, t * LANES : (t + 1) * LANES] for t in range(4)]
+            pieces = [jnp.where(step_one, pieces[(t + 1) % 4], pieces[t]) for t in range(4)]
+            pieces = [jnp.where(step_two, pieces[(t + 2) % 4], pieces[t]) for t in range(4)]
+            for piece, out_ref in zip(pieces, out_refs, strict=True):
+                out_ref[pl.ds(c * block + k, rows, stride=own), :] = piece
+        return carry
+
+    lax.fori_loop(0, own // 2, lambda pair, carry: each(2 * pair + 1, each(2 * pair, carry)), 0)
+
+
+def integral_kernel(limits_ref, energy_ref, parts_ref, *refs):
+    *out_refs, split_ref = refs
+    integral_into(limits_ref, energy_ref, parts_ref, out_refs, split_ref)
+
+
+def first_integral_kernel(limits_ref, energy_ref, stored_ref, *refs):
+    *out_refs, parts_ref, split_ref, buffer_ref, arrived = refs
+    kinds, halves, own, times, _ = stored_ref.shape
+
+    def fetch(k, n):
+        source = stored_ref.at[n // halves, n % halves, k]
+        return pltpu.make_async_copy(source, buffer_ref.at[k, n], arrived.at[k, n])
+
+    for k in range(own):
+        for n in range(kinds * halves):
+            fetch(k, n).start()
+
+    def prepare(k):
+        for n in range(kinds * halves):
+            fetch(k, n).wait()
+            high, low = split_high_low(buffer_ref[k, n])
+            parts_ref[0, k, n * times : (n + 1) * times, :] = high
+            parts_ref[1, k, n * times : (n + 1) * times, :] = low
+
+    integral_into(limits_ref, energy_ref, parts_ref, out_refs, split_ref, prepare)
+
+
+def slope_of(parts, state, band_ref):
     block = band_ref.shape[0]
-    total = parts_ref[0]
-    for t in range(1, parts_ref.shape[0]):
-        total = total + parts_ref[t]
+    total = (parts[0][...] + parts[1][...]) + (parts[2][...] + parts[3][...])
     packed = swap_groups([total[c * block : (c + 1) * block] for c in range(4)])
     band = band_ref[...]
     return jnp.concatenate(
@@ -180,20 +194,20 @@
     )
 
 
-def predict_kernel(parts_ref, state_ref, band_ref, out_ref, base_ref):
+def predict_kernel(own_ref, one_ref, two_ref, three_ref, state_ref, band_ref, out_ref, base_ref):
     state = state_ref[...]
-    slope = slope_of(parts_ref, state, band_ref)
+    slope = slope_of((own_ref, one_ref, two_ref, three_ref), state, band_ref)
     out_ref[...] = state + TIME_STEP * slope
     base_ref[...] = state + (0.5 * TIME_STEP) * slope
 
 
-def correct_kernel(parts_ref, state_ref, band_ref, base_ref, out_ref):
-    slope = slope_of(parts_ref, state_ref[...], band_ref)
+def correct_kernel(own_ref, one_ref, two_ref, three_ref, state_ref, band_ref, base_ref, out_ref):
+    slope = slope_of((own_ref, one_ref, two_ref, three_ref), state_ref[...], band_ref)
     out_ref[...] = base_ref[...] + (0.5 * TIME_STEP) * slope
 
 
-def last_kernel(parts_ref, state_ref, band_ref, base_ref, out_ref, split_ref):
-    slope = slope_of(parts_ref, state_ref[...], band_ref)
+def last_kernel(own_ref, one_ref, two_ref, three_ref, state_ref, band_ref, base_ref, out_ref, split_ref):
+    slope = slope_of((own_ref, one_ref, two_ref, three_ref), state_ref[...], band_ref)
     value = base_ref[...] + (0.5 * TIME_STEP) * slope
     block = band_ref.shape[0]
     parts = swap_groups([value[q * block : (q + 1) * block] for q in range(4)])
@@ -237,58 +251,59 @@
     own_map = lax.dynamic_slice_in_dim(momentum_map, lax.axis_index("mom") * own, own, 0)
     first_times = step_index[0].astype(F32) + jnp.arange(row_count, dtype=jnp.int32).astype(F32)
     bands = [band_rows(own_map, first_times, float(offset)) for offset in range(3)]
-    limits = jnp.stack([lax.axis_index("tm") * time_count, history_len[0]])
+    limits = jnp.stack([lax.axis_index("tm"), history_len[0]])
 
     vmem = pltpu.VMEM
     pack = resident(pack_kernel, [packed_shape], [vmem], "pack")
     stored = 6 * time_count
-    split_shape = jax.ShapeDtypeStruct((own, stored, hist), BF16)
-    split_history = resident(
-        history_kernel,
-        [split_shape] * 2,
-        [pltpu.HBM],
-        "split_history",
-        [vmem((3, *history.shape[2:]), F32), pltpu.SemaphoreType.DMA((3,))],
-        5 << 20,
-    )
+    parts_shape = jax.ShapeDtypeStruct((2, own, stored, hist), BF16)
     site = resident(site_kernel, [packed_shape], [vmem] * 2, "site")
     tm_size = lax.axis_size("tm")
-    parts_shape = jax.ShapeDtypeStruct((tm_size, 4 * block, LANES), F32)
+    split_scratch = vmem((4, block, LANES), F32)
     integral = resident(
-        integral_kernel, [parts_shape], [pltpu.SMEM] + [vmem] * 3, "integral", [vmem((4, block, LANES), F32)]
-    )
-    predict = resident(predict_kernel, [packed_shape] * 2, [vmem] * 3, "predict")
-    correct = resident(correct_kernel, [packed_shape], [vmem] * 4, "correct")
-    last = pl.pallas_call(
-        last_kernel,
-        out_shape=jax.ShapeDtypeStruct(new_rows.shape, F32),
-        scratch_shapes=[pltpu.VMEM((4, block, LANES), F32)],
-        name="last",
-    )
-
+        integral_kernel, [packed_shape] * tm_size, [pltpu.SMEM, vmem, vmem], "integral", [split_scratch]
+    )
+    first_integral = resident(
+        first_integral_kernel,
+        [packed_shape] * tm_size + [parts_shape],
+        [pltpu.SMEM, vmem, pltpu.HBM],
+        "first_integral",
+        [split_scratch, vmem((own, 6, time_count, hist), F32), pltpu.SemaphoreType.DMA((own, 6))],
+        9 << 20,
+    )
+    predict = resident(predict_kernel, [packed_shape] * 2, [vmem] * 6, "predict")
+    correct = resident(correct_kernel, [packed_shape], [vmem] * 7, "correct")
+    last = resident(
+        last_kernel, [jax.ShapeDtypeStruct(new_rows.shape, F32)], [vmem] * 7, "last", [split_scratch]
+    )
     (state,) = pack(new_rows)
-    high, low = split_history(history)
 
     def turned(value):
         return lax.all_to_all(value, "mom", 0, 0, tiled=True)
 
-    def parts_of(arrived):
+    def exchange(partial):
+        hops = {n: [(t, (t + n) % tm_size) for t in range(tm_size)] for n in (2, 1, 3)}
+        parts = {n: lax.ppermute(partial[n], "tm", hop) for n, hop in hops.items()}
+        return partial[0], parts[2], parts[1], parts[3]
+
+    def energy_of(arrived):
         (energy,) = site(table, arrived)
-        (partial,) = integral(limits, turned(energy), high, low)
-        return lax.all_to_all(partial, "tm", 0, 0, tiled=True)
+        return turned(energy)
 
     first = turned(state)
-    first, table, high, low, limits, bands, state = lax.optimization_barrier(
-        (first, table, high, low, limits, bands, state)
-    )
+    first, limits, bands = lax.optimization_barrier((first, limits, bands))
+    *partial, stored_parts = first_integral(limits, energy_of(first), history)
+
+    def parts_of(estimate):
+        return exchange(integral(limits, energy_of(turned(estimate)), stored_parts))
 
     for time_step in range(2):
-        arrived = first if time_step == 0 else turned(state)
-        estimate, base = predict(parts_of(arrived), state, bands[time_step])
-        (estimate,) = correct(parts_of(turned(estimate)), estimate, bands[time_step + 1], base)
+        parts = exchange(partial) if time_step == 0 else parts_of(state)
+        estimate, base = predict(*parts, state, bands[time_step])
+        (estimate,) = correct(*parts_of(estimate), estimate, bands[time_step + 1], base)
         if time_step == 0:
-            (state,) = correct(parts_of(turned(estimate)), estimate, bands[time_step + 1], base)
-    return last(parts_of(turned(estimate)), estimate, bands[2], base)
+            (state,) = correct(*parts_of(estimate), estimate, bands[1], base)
+    return last(*parts_of(estimate), estimate, bands[2], base)[0]
 
 
 def solution(mesh):

time: 300 us -> 275 us (0.917)
  blocking collectives: 247 us -> 166 us
  waiting for transfers between devices: 0.01 us -> 37.1 us
  starting transfers between devices: 13 us -> 40.3 us
  local copies, waits for them, and re-layouts: 5.99 us -> 2.03 us
    all_to_all x6 -> x0, blocking collectives: 71.3 us -> none  [parts_of(): return lax.all_to_all(partial, 'tm', 0, 0, tiled=True)]
    ppermute x0 -> x18, waiting for transfers between devices: none -> 30.8 us  [exchange(): parts = {n: lax.ppermute(partial[n], 'tm', hop) for n, hop in hops.items()}]
    ppermute x0 -> x18, starting transfers between devices: none -> 27.3 us  [exchange(): parts = {n: lax.ppermute(partial[n], 'tm', hop) for n, hop in hops.items()}]
    all_to_all x11, blocking collectives: 175 us -> 166 us  [turned(): return lax.all_to_all(value, 'mom', 0, 0, tiled=True)]
    all_to_all x1, waiting for transfers between devices: 0.01 us -> 6.32 us  [turned(): return lax.all_to_all(value, 'mom', 0, 0, tiled=True)]
    unnamed x18 -> x3, local copies, waits for them, and re-layouts: 5.52 us -> 1.56 us
  transfers between devices with their start and end apart: 1 -> 19, of which waited for: 0 -> 13; matrix products, arithmetic and copies ran while one was open for 2% -> 1% of each run, Pallas kernels for 1% -> 0%
where the time goes in v2:
time: 275 us; the launch traced here: 274 us
  blocking collectives  166 us (60%)
  starting transfers between devices  40.3 us (15%)
  waiting for transfers between devices  37.1 us (13%)
  Pallas kernels  24.3 us (9%)
  other arithmetic  3.17 us (1%)
    all_to_all x11, blocking collectives, turned(): return lax.all_to_all(value, 'mom', 0, 0, tiled=True)  166 us
    ppermute x18, waiting for transfers between devices, exchange(): parts = {n: lax.ppermute(partial[n], 'tm', hop) for n, hop in hops.items()}  30.8 us
    ppermute x18, starting transfers between devices, exchange(): parts = {n: lax.ppermute(partial[n], 'tm', hop) for n, hop in hops.items()}  27.3 us
    pallas_call x19, Pallas kernels, apply(): return call(*placed)  24.3 us
    all_to_all x1, starting transfers between devices, turned(): return lax.all_to_all(value, 'mom', 0, 0, tiled=True)  13 us
    all_to_all x1, waiting for transfers between devices, turned(): return lax.all_to_all(value, 'mom', 0, 0, tiled=True)  6.32 us
  transfers between devices with their start and end apart: 19, of which 13 were waited for; matrix products, arithmetic and copies ran while one was open for 1% of the time, Pallas kernels for 0%

profile of v2, /device:TPU:1, one launch (start us, length us, event | category | flops | bytes accessed | tf_op | source)
XLA Modules:
  0.0 274.5 jit_solution(17711014445672658984)
XLA Ops:
  1.7 13.0 %all-to-all-start = ((f32[64,4,128]{2,1,0:T(4,128)}), f32[64,4,128]{2,1,0:T(4,128)S(1)}, u32[]{:S(2)}, u32[]{:S(2)}) async-start(f32[64,4,128]{2,1,0:T(4,128)} %bitcast), calls=%async_computation | async-start | bytes 262144 | tf_op jit(solution)/shard_map/all_to_all | solution.py:282
  19.5 6.3 %all-to-all-done = f32[64,4,128]{2,1,0:T(4,128)S(1)} async-done(((f32[64,4,128]{2,1,0:T(4,128)}), f32[64,4,128]{2,1,0:T(4,128)S(1)}, u32[]{:S(2)}, u32[]{:S(2)}) %all-to-all-start) | async-done | bytes 131104 | tf_op jit(solution)/shard_map/all_to_all | solution.py:282
  27.2 14.9 %all_to_all.133 = f32[64,4,128]{2,1,0:T(4,128)S(1)} all-to-all(f32[64,4,128]{2,1,0:T(4,128)S(1)} %bitcast.37), channel_id=1, replica_groups=mesh['mom'=64,'tm'=4] {'mom'}, dimensions={0} | all-to-all | bytes 262144 | tf_op jit(solution)/shard_map/all_to_all | solution.py:282
  42.1 4.3 %first_integral.1 = (f32[256,128]{1,0:T(8,128)S(1)}, f32[256,128]{1,0:T(8,128)S(1)}, f32[256,128]{1,0:T(8,128)S(1)}, f32[256,128]{1,0:T(8,128)S(1)}, bf16[2,4,768,512]{3,2,1,0:T(8,128)(2,1)S(1)}) custom-call(s32[2]{0:T(128)S(1)} %pad_add_fusion.limits_ref, f32[256,128]{1,0:T(8,128)S(1)} %bitcast.30, f32[3,2,4,128,512]{4,3,2,1,0:T(8,128)} %stored_ref.1), custom_call_target="tpu_custom_call" | custom-call | tf_op jit(solution)/shard_map/first_integral/pallas_call | solution.py:65
  46.4 3.0 %collective-permute-start = (f32[256,128]{1,0:T(8,128)S(1)}, f32[256,128]{1,0:T(8,128)S(1)}, u32[]{:S(2)}, u32[]{:S(2)}) collective-permute-start(f32[256,128]{1,0:T(8,128)S(1)} %get-tuple-element.42), channel_id=1, source_target_pairs={{0,2},{1,3},{2,0},{3,1},{4,6},{5,7},{6,4},{7,5},{8,10},{9,11},{10,... | collective-permute-start | bytes 393224 | tf_op jit(solution)/shard_map/ppermute | solution.py:286
  49.8 2.3 collective-permute-start.2
  52.7 3.3 %collective-permute-done.1.two_ref = f32[256,128]{1,0:T(8,128)S(1)} collective-permute-done((f32[256,128]{1,0:T(8,128)S(1)}, f32[256,128]{1,0:T(8,128)S(1)}, u32[]{:S(2)}, u32[]{:S(2)}) %collective-permute-start.1) | collective-permute-done | bytes 131104 | tf_op jit(solution)/shard_map/ppermute | solution.py:286
  57.2 15.6 %all_to_all.134 = f32[64,4,128]{2,1,0:T(4,128)S(1)} all-to-all(f32[64,4,128]{2,1,0:T(4,128)S(1)} %bitcast.47), channel_id=1, replica_groups=mesh['mom'=64,'tm'=4] {'mom'}, dimensions={0} | all-to-all | bytes 262144 | tf_op jit(solution)/shard_map/all_to_all | solution.py:282
  73.9 14.9 %all_to_all.135 = f32[64,4,128]{2,1,0:T(4,128)S(1)} all-to-all(f32[64,4,128]{2,1,0:T(4,128)S(1)} %bitcast.38), channel_id=1, replica_groups=mesh['mom'=64,'tm'=4] {'mom'}, dimensions={0} | all-to-all | bytes 262144 | tf_op jit(solution)/shard_map/all_to_all | solution.py:282
  97.1 3.3 %collective-permute-done.4.two_ref = f32[256,128]{1,0:T(8,128)S(1)} collective-permute-done((f32[256,128]{1,0:T(8,128)S(1)}, f32[256,128]{1,0:T(8,128)S(1)}, u32[]{:S(2)}, u32[]{:S(2)}) %collective-permute-start.4) | collective-permute-done | bytes 131104 | tf_op jit(solution)/shard_map/ppermute | solution.py:286
  100.7 15.6 %all_to_all.136 = f32[64,4,128]{2,1,0:T(4,128)S(1)} all-to-all(f32[64,4,128]{2,1,0:T(4,128)S(1)} %bitcast.28), channel_id=1, replica_groups=mesh['mom'=64,'tm'=4] {'mom'}, dimensions={0} | all-to-all | bytes 262144 | tf_op jit(solution)/shard_map/all_to_all | solution.py:282
  117.4 14.9 %all_to_all.137 = f32[64,4,128]{2,1,0:T(4,128)S(1)} all-to-all(f32[64,4,128]{2,1,0:T(4,128)S(1)} %bitcast.39), channel_id=1, replica_groups=mesh['mom'=64,'tm'=4] {'mom'}, dimensions={0} | all-to-all | bytes 262144 | tf_op jit(solution)/shard_map/all_to_all | solution.py:282
  138.5 2.0 collective-permute-done.6.one_ref
  140.5 3.5 %collective-permute-done.7.two_ref = f32[256,128]{1,0:T(8,128)S(1)} collective-permute-done((f32[256,128]{1,0:T(8,128)S(1)}, f32[256,128]{1,0:T(8,128)S(1)}, u32[]{:S(2)}, u32[]{:S(2)}) %collective-permute-start.7) | collective-permute-done | bytes 131104 | tf_op jit(solution)/shard_map/ppermute | solution.py:286
  144.2 15.1 %all_to_all.138 = f32[64,4,128]{2,1,0:T(4,128)S(1)} all-to-all(f32[64,4,128]{2,1,0:T(4,128)S(1)} %bitcast.26), channel_id=1, replica_groups=mesh['mom'=64,'tm'=4] {'mom'}, dimensions={0} | all-to-all | bytes 262144 | tf_op jit(solution)/shard_map/all_to_all | solution.py:282
  160.4 14.9 %all_to_all.139 = f32[64,4,128]{2,1,0:T(4,128)S(1)} all-to-all(f32[64,4,128]{2,1,0:T(4,128)S(1)} %bitcast.40), channel_id=1, replica_groups=mesh['mom'=64,'tm'=4] {'mom'}, dimensions={0} | all-to-all | bytes 262144 | tf_op jit(solution)/shard_map/all_to_all | solution.py:282
  181.6 2.0 collective-permute-done.9.one_ref
  183.6 3.5 %collective-permute-done.10.two_ref = f32[256,128]{1,0:T(8,128)S(1)} collective-permute-done((f32[256,128]{1,0:T(8,128)S(1)}, f32[256,128]{1,0:T(8,128)S(1)}, u32[]{:S(2)}, u32[]{:S(2)}) %collective-permute-start.10) | collective-permute-done | bytes 131104 | tf_op jit(solution)/shard_map/ppermute | solution.py:286
  187.3 15.4 %all_to_all.140 = f32[64,4,128]{2,1,0:T(4,128)S(1)} all-to-all(f32[64,4,128]{2,1,0:T(4,128)S(1)} %bitcast.48), channel_id=1, replica_groups=mesh['mom'=64,'tm'=4] {'mom'}, dimensions={0} | all-to-all | bytes 262144 | tf_op jit(solution)/shard_map/all_to_all | solution.py:282
  203.8 14.9 %all_to_all.141 = f32[64,4,128]{2,1,0:T(4,128)S(1)} all-to-all(f32[64,4,128]{2,1,0:T(4,128)S(1)} %bitcast.41), channel_id=1, replica_groups=mesh['mom'=64,'tm'=4] {'mom'}, dimensions={0} | all-to-all | bytes 262144 | tf_op jit(solution)/shard_map/all_to_all | solution.py:282
  226.9 3.5 %collective-permute-done.13.two_ref = f32[256,128]{1,0:T(8,128)S(1)} collective-permute-done((f32[256,128]{1,0:T(8,128)S(1)}, f32[256,128]{1,0:T(8,128)S(1)}, u32[]{:S(2)}, u32[]{:S(2)}) %collective-permute-start.13) | collective-permute-done | bytes 131104 | tf_op jit(solution)/shard_map/ppermute | solution.py:286
  230.6 15.1 %all_to_all.142 = f32[64,4,128]{2,1,0:T(4,128)S(1)} all-to-all(f32[64,4,128]{2,1,0:T(4,128)S(1)} %bitcast.27), channel_id=1, replica_groups=mesh['mom'=64,'tm'=4] {'mom'}, dimensions={0} | all-to-all | bytes 262144 | tf_op jit(solution)/shard_map/all_to_all | solution.py:282
  246.8 14.9 %all_to_all.143 = f32[64,4,128]{2,1,0:T(4,128)S(1)} all-to-all(f32[64,4,128]{2,1,0:T(4,128)S(1)} %bitcast.36), channel_id=1, replica_groups=mesh['mom'=64,'tm'=4] {'mom'}, dimensions={0} | all-to-all | bytes 262144 | tf_op jit(solution)/shard_map/all_to_all | solution.py:282
  270.0 3.5 %collective-permute-done.16.two_ref = f32[256,128]{1,0:T(8,128)S(1)} collective-permute-done((f32[256,128]{1,0:T(8,128)S(1)}, f32[256,128]{1,0:T(8,128)S(1)}, u32[]{:S(2)}, u32[]{:S(2)}) %collective-permute-start.16) | collective-permute-done | bytes 131104 | tf_op jit(solution)/shard_map/ppermute | solution.py:286
  (62 shorter events, 53.5 us)
Async XLA Ops:
  0.0 0.9 copy-start
  1.7 24.1 %all-to-all-start = ((f32[64,4,128]{2,1,0:T(4,128)}), f32[64,4,128]{2,1,0:T(4,128)S(1)}, u32[]{:S(2)}, u32[]{:S(2)}) async-start(f32[64,4,128]{2,1,0:T(4,128)} %bitcast), calls=%async_computation | async-start | bytes 262144 | tf_op jit(solution)/shard_map/all_to_all | solution.py:282
  46.4 6.3 %collective-permute-start = (f32[256,128]{1,0:T(8,128)S(1)}, f32[256,128]{1,0:T(8,128)S(1)}, u32[]{:S(2)}, u32[]{:S(2)}) collective-permute-start(f32[256,128]{1,0:T(8,128)S(1)} %get-tuple-element.42), channel_id=1, source_target_pairs={{0,2},{1,3},{2,0},{3,1},{4,6},{5,7},{6,4},{7,5},{8,10},{9,11},{10,... | collective-permute-start | bytes 393224 | tf_op jit(solution)/shard_map/ppermute | solution.py:286
  49.4 6.6 %collective-permute-start.1 = (f32[256,128]{1,0:T(8,128)S(1)}, f32[256,128]{1,0:T(8,128)S(1)}, u32[]{:S(2)}, u32[]{:S(2)}) collective-permute-start(f32[256,128]{1,0:T(8,128)S(1)} %get-tuple-element.43), channel_id=1, source_target_pairs={{0,1},{1,2},{2,3},{3,0},{4,5},{5,6},{6,7},{7,4},{8,9},{9,10},{10,1... | collective-permute-start | bytes 393224 | tf_op jit(solution)/shard_map/ppermute | solution.py:286
  49.8 6.2 %collective-permute-start.2 = (f32[256,128]{1,0:T(8,128)S(1)}, f32[256,128]{1,0:T(8,128)S(1)}, u32[]{:S(2)}, u32[]{:S(2)}) collective-permute-start(f32[256,128]{1,0:T(8,128)S(1)} %get-tuple-element.44), channel_id=1, source_target_pairs={{0,3},{1,0},{2,1},{3,2},{4,7},{5,4},{6,5},{7,6},{8,11},{9,8},{10,9... | collective-permute-start | bytes 393224 | tf_op jit(solution)/shard_map/ppermute | solution.py:286
  90.8 6.3 %collective-permute-start.3 = (f32[256,128]{1,0:T(8,128)S(1)}, f32[256,128]{1,0:T(8,128)S(1)}, u32[]{:S(2)}, u32[]{:S(2)}) collective-permute-start(f32[256,128]{1,0:T(8,128)S(1)} %get-tuple-element.49), channel_id=1, source_target_pairs={{0,2},{1,3},{2,0},{3,1},{4,6},{5,7},{6,4},{7,5},{8,10},{9,11},{10,... | collective-permute-start | bytes 393224 | tf_op jit(solution)/shard_map/ppermute | solution.py:286
  92.7 7.7 %collective-permute-start.4 = (f32[256,128]{1,0:T(8,128)S(1)}, f32[256,128]{1,0:T(8,128)S(1)}, u32[]{:S(2)}, u32[]{:S(2)}) collective-permute-start(f32[256,128]{1,0:T(8,128)S(1)} %get-tuple-element.50), channel_id=1, source_target_pairs={{0,1},{1,2},{2,3},{3,0},{4,5},{5,6},{6,7},{7,4},{8,9},{9,10},{10,1... | collective-permute-start | bytes 393224 | tf_op jit(solution)/shard_map/ppermute | solution.py:286
  94.2 6.2 %collective-permute-start.5 = (f32[256,128]{1,0:T(8,128)S(1)}, f32[256,128]{1,0:T(8,128)S(1)}, u32[]{:S(2)}, u32[]{:S(2)}) collective-permute-start(f32[256,128]{1,0:T(8,128)S(1)} %get-tuple-element.51), channel_id=1, source_target_pairs={{0,3},{1,0},{2,1},{3,2},{4,7},{5,4},{6,5},{7,6},{8,11},{9,8},{10,9... | collective-permute-start | bytes 393224 | tf_op jit(solution)/shard_map/ppermute | solution.py:286
  134.2 6.3 %collective-permute-start.6 = (f32[256,128]{1,0:T(8,128)S(1)}, f32[256,128]{1,0:T(8,128)S(1)}, u32[]{:S(2)}, u32[]{:S(2)}) collective-permute-start(f32[256,128]{1,0:T(8,128)S(1)} %get-tuple-element.55), channel_id=1, source_target_pairs={{0,2},{1,3},{2,0},{3,1},{4,6},{5,7},{6,4},{7,5},{8,10},{9,11},{10,... | collective-permute-start | bytes 393224 | tf_op jit(solution)/shard_map/ppermute | solution.py:286
  135.8 8.1 %collective-permute-start.7 = (f32[256,128]{1,0:T(8,128)S(1)}, f32[256,128]{1,0:T(8,128)S(1)}, u32[]{:S(2)}, u32[]{:S(2)}) collective-permute-start(f32[256,128]{1,0:T(8,128)S(1)} %get-tuple-element.56), channel_id=1, source_target_pairs={{0,1},{1,2},{2,3},{3,0},{4,5},{5,6},{6,7},{7,4},{8,9},{9,10},{10,1... | collective-permute-start | bytes 393224 | tf_op jit(solution)/shard_map/ppermute | solution.py:286
  137.3 6.7 %collective-permute-start.8 = (f32[256,128]{1,0:T(8,128)S(1)}, f32[256,128]{1,0:T(8,128)S(1)}, u32[]{:S(2)}, u32[]{:S(2)}) collective-permute-start(f32[256,128]{1,0:T(8,128)S(1)} %get-tuple-element.57), channel_id=1, source_target_pairs={{0,3},{1,0},{2,1},{3,2},{4,7},{5,4},{6,5},{7,6},{8,11},{9,8},{10,9... | collective-permute-start | bytes 393224 | tf_op jit(solution)/shard_map/ppermute | solution.py:286
  177.3 6.3 %collective-permute-start.9 = (f32[256,128]{1,0:T(8,128)S(1)}, f32[256,128]{1,0:T(8,128)S(1)}, u32[]{:S(2)}, u32[]{:S(2)}) collective-permute-start(f32[256,128]{1,0:T(8,128)S(1)} %get-tuple-element.59), channel_id=1, source_target_pairs={{0,2},{1,3},{2,0},{3,1},{4,6},{5,7},{6,4},{7,5},{8,10},{9,11},{10,... | collective-permute-start | bytes 393224 | tf_op jit(solution)/shard_map/ppermute | solution.py:286
  178.9 8.1 %collective-permute-start.10 = (f32[256,128]{1,0:T(8,128)S(1)}, f32[256,128]{1,0:T(8,128)S(1)}, u32[]{:S(2)}, u32[]{:S(2)}) collective-permute-start(f32[256,128]{1,0:T(8,128)S(1)} %get-tuple-element.60), channel_id=1, source_target_pairs={{0,1},{1,2},{2,3},{3,0},{4,5},{5,6},{6,7},{7,4},{8,9},{9,10},{10,1... | collective-permute-start | bytes 393224 | tf_op jit(solution)/shard_map/ppermute | solution.py:286
  180.3 6.7 %collective-permute-start.11 = (f32[256,128]{1,0:T(8,128)S(1)}, f32[256,128]{1,0:T(8,128)S(1)}, u32[]{:S(2)}, u32[]{:S(2)}) collective-permute-start(f32[256,128]{1,0:T(8,128)S(1)} %get-tuple-element.61), channel_id=1, source_target_pairs={{0,3},{1,0},{2,1},{3,2},{4,7},{5,4},{6,5},{7,6},{8,11},{9,8},{10,9... | collective-permute-start | bytes 393224 | tf_op jit(solution)/shard_map/ppermute | solution.py:286
  220.6 6.3 %collective-permute-start.12 = (f32[256,128]{1,0:T(8,128)S(1)}, f32[256,128]{1,0:T(8,128)S(1)}, u32[]{:S(2)}, u32[]{:S(2)}) collective-permute-start(f32[256,128]{1,0:T(8,128)S(1)} %get-tuple-element.64), channel_id=1, source_target_pairs={{0,2},{1,3},{2,0},{3,1},{4,6},{5,7},{6,4},{7,5},{8,10},{9,11},{10,... | collective-permute-start | bytes 393224 | tf_op jit(solution)/shard_map/ppermute | solution.py:286
  222.2 8.1 %collective-permute-start.13 = (f32[256,128]{1,0:T(8,128)S(1)}, f32[256,128]{1,0:T(8,128)S(1)}, u32[]{:S(2)}, u32[]{:S(2)}) collective-permute-start(f32[256,128]{1,0:T(8,128)S(1)} %get-tuple-element.65), channel_id=1, source_target_pairs={{0,1},{1,2},{2,3},{3,0},{4,5},{5,6},{6,7},{7,4},{8,9},{9,10},{10,1... | collective-permute-start | bytes 393224 | tf_op jit(solution)/shard_map/ppermute | solution.py:286
  223.7 6.7 %collective-permute-start.14 = (f32[256,128]{1,0:T(8,128)S(1)}, f32[256,128]{1,0:T(8,128)S(1)}, u32[]{:S(2)}, u32[]{:S(2)}) collective-permute-start(f32[256,128]{1,0:T(8,128)S(1)} %get-tuple-element.66), channel_id=1, source_target_pairs={{0,3},{1,0},{2,1},{3,2},{4,7},{5,4},{6,5},{7,6},{8,11},{9,8},{10,9... | collective-permute-start | bytes 393224 | tf_op jit(solution)/shard_map/ppermute | solution.py:286
  263.7 6.3 %collective-permute-start.15 = (f32[256,128]{1,0:T(8,128)S(1)}, f32[256,128]{1,0:T(8,128)S(1)}, u32[]{:S(2)}, u32[]{:S(2)}) collective-permute-start(f32[256,128]{1,0:T(8,128)S(1)} %get-tuple-element.70), channel_id=1, source_target_pairs={{0,2},{1,3},{2,0},{3,1},{4,6},{5,7},{6,4},{7,5},{8,10},{9,11},{10,... | collective-permute-start | bytes 393224 | tf_op jit(solution)/shard_map/ppermute | solution.py:286
  265.3 8.1 %collective-permute-start.16 = (f32[256,128]{1,0:T(8,128)S(1)}, f32[256,128]{1,0:T(8,128)S(1)}, u32[]{:S(2)}, u32[]{:S(2)}) collective-permute-start(f32[256,128]{1,0:T(8,128)S(1)} %get-tuple-element.71), channel_id=1, source_target_pairs={{0,1},{1,2},{2,3},{3,0},{4,5},{5,6},{6,7},{7,4},{8,9},{9,10},{10,1... | collective-permute-start | bytes 393224 | tf_op jit(solution)/shard_map/ppermute | solution.py:286
  266.7 6.7 %collective-permute-start.17 = (f32[256,128]{1,0:T(8,128)S(1)}, f32[256,128]{1,0:T(8,128)S(1)}, u32[]{:S(2)}, u32[]{:S(2)}) collective-permute-start(f32[256,128]{1,0:T(8,128)S(1)} %get-tuple-element.72), channel_id=1, source_target_pairs={{0,3},{1,0},{2,1},{3,2},{4,7},{5,4},{6,5},{7,6},{8,11},{9,8},{10,9... | collective-permute-start | bytes 393224 | tf_op jit(solution)/shard_map/ppermute | solution.py:286

commit v3 on v2

--- a/solution.py
+++ b/solution.py
@@ -45,7 +45,7 @@
     return jnp.where(even, pltpu.roll(value, LANES - GROUP, 1), -pltpu.roll(value, GROUP, 1))
 
 
-def resident(kernel, out_shapes, in_spaces, name, scratch=(), limit=4 << 20):
+def resident(kernel, out_shapes, in_spaces, name, scratch=(), limit=4 << 20, cost=None):
     results = [pltpu.VMEM(o.shape, o.dtype) for o in out_shapes]
     call = pl.pallas_call(
         kernel,
@@ -54,6 +54,7 @@
         out_shape=results,
         scratch_shapes=scratch,
         compiler_params=pltpu.CompilerParams(vmem_limit_bytes=limit),
+        cost_estimate=cost,
         name=name,
     )
 
@@ -86,9 +87,9 @@
         ],
         axis=0,
     )
-    depth = operand.shape[0]
-    total = jnp.dot(table_ref[:, :depth], operand, preferred_element_type=F32)
-    total = total + jnp.dot(table_ref[:, depth:], operand, preferred_element_type=F32)
+    count = value.shape[0]
+    total = jnp.dot(table_ref[...], operand, preferred_element_type=F32)
+    total = total[:count] + total[count:]
     return total[:, :LANES] + total[:, LANES:]
 
 
@@ -112,10 +113,12 @@
     out_ref[...] = transform(table_ref, energy, times_minus_i(energy))
 
 
-def integral_into(limits_ref, energy_ref, parts_ref, out_refs, split_ref, prepare=None):
-    step_one = limits_ref[0] % 2 == 1
-    step_two = limits_ref[0] // 2 == 1
-    own = parts_ref.shape[1]
+PLACES = (2, 1, 3, 0)
+FAR = 1
+
+
+def left_factors(limits_ref, energy_ref, left_ref, split_ref):
+    own = left_ref.shape[0]
     block = split_ref.shape[1]
     rows = block // own
     position = limits_ref[0] * LANES + lax.broadcasted_iota(jnp.int32, (block, LANES), 1)
@@ -123,47 +126,58 @@
     parts = swap_groups([energy_ref[q * block : (q + 1) * block, :] for q in range(4)])
     for c in range(4):
         split_ref[c] = parts[c] * mask
-
-    def left(k, pair):
-        real = split_ref[2 * pair, pl.ds(k, rows, stride=own), :]
-        imag = split_ref[2 * pair + 1, pl.ds(k, rows, stride=own), :]
-        joined = jnp.concatenate(
-            [jnp.concatenate([real, -imag], axis=1), jnp.concatenate([imag, real], axis=1)], axis=0
-        )
-        high, low = split_high_low(joined)
-        return jnp.concatenate([high, low], axis=0)
-
-    def product(k, lhs, start, stop):
-        both = jnp.dot(lhs, parts_ref[0, k, start:stop, :], preferred_element_type=F32)
-        small = jnp.dot(lhs[: 2 * rows], parts_ref[1, k, start:stop, :], preferred_element_type=F32)
-        return TIME_STEP * (both[: 2 * rows] + both[2 * rows :] + small)
+    for k in range(own):
+        for pair in range(2):
+            real = split_ref[2 * pair, pl.ds(k, rows, stride=own), :]
+            imag = split_ref[2 * pair + 1, pl.ds(k, rows, stride=own), :]
+            joined = jnp.concatenate(
+                [jnp.concatenate([real, -imag], axis=1), jnp.concatenate([imag, real], axis=1)], axis=0
+            )
+            high, low = split_high_low(joined)
+            columns = slice(2 * pair * LANES, 2 * (pair + 1) * LANES)
+            left_ref[k, : 2 * rows, columns] = high
+            left_ref[k, 2 * rows :, columns] = low
+
+
+def products_into(left_ref, parts_ref, out_refs, first, prepare=None):
+    own = left_ref.shape[0]
+    rows = left_ref.shape[1] // 4
+    block = own * rows
+    columns = slice(first * LANES, (first + len(out_refs)) * LANES)
 
     def each(k, carry):
         if prepare is not None:
             prepare(k)
-        retarded_left = left(k, 0)
-        lesser_left = jnp.concatenate([retarded_left, left(k, 1)], axis=1)
-        retarded = product(k, retarded_left, 0, 2 * LANES)
-        lesser = product(k, lesser_left, 2 * LANES, 6 * LANES)
+
+        def product(lhs, start, stop):
+            both = jnp.dot(lhs, parts_ref[0, k, start:stop, columns], preferred_element_type=F32)
+            small = jnp.dot(lhs[: 2 * rows], parts_ref[1, k, start:stop, columns], preferred_element_type=F32)
+            return TIME_STEP * (both[: 2 * rows] + both[2 * rows :] + small)
+
+        left = left_ref[k]
+        retarded = product(left[:, : 2 * LANES], 0, 2 * LANES)
+        lesser = product(left, 2 * LANES, 6 * LANES)
         values = (retarded[:rows], retarded[rows:], lesser[:rows], lesser[rows:])
         for c, value in enumerate(values):
-            pieces = [value[:, t * LANES : (t + 1) * LANES] for t in range(4)]
-            pieces = [jnp.where(step_one, pieces[(t + 1) % 4], pieces[t]) for t in range(4)]
-            pieces = [jnp.where(step_two, pieces[(t + 2) % 4], pieces[t]) for t in range(4)]
-            for piece, out_ref in zip(pieces, out_refs, strict=True):
-                out_ref[pl.ds(c * block + k, rows, stride=own), :] = piece
+            for n, out_ref in enumerate(out_refs):
+                out_ref[pl.ds(c * block + k, rows, stride=own), :] = value[:, n * LANES : (n + 1) * LANES]
         return carry
 
     lax.fori_loop(0, own // 2, lambda pair, carry: each(2 * pair + 1, each(2 * pair, carry)), 0)
 
 
-def integral_kernel(limits_ref, energy_ref, parts_ref, *refs):
-    *out_refs, split_ref = refs
-    integral_into(limits_ref, energy_ref, parts_ref, out_refs, split_ref)
+def far_integral_kernel(limits_ref, energy_ref, parts_ref, *refs):
+    *out_refs, left_ref, split_ref = refs
+    left_factors(limits_ref, energy_ref, left_ref, split_ref)
+    products_into(left_ref, parts_ref, out_refs, 0)
+
+
+def near_integral_kernel(left_ref, parts_ref, *out_refs):
+    products_into(left_ref, parts_ref, out_refs, len(PLACES) - len(out_refs))
 
 
 def first_integral_kernel(limits_ref, energy_ref, stored_ref, *refs):
-    *out_refs, parts_ref, split_ref, buffer_ref, arrived = refs
+    *out_refs, parts_ref, left_ref, split_ref, buffer_ref, arrived = refs
     kinds, halves, own, times, _ = stored_ref.shape
 
     def fetch(k, n):
@@ -174,14 +188,19 @@
         for n in range(kinds * halves):
             fetch(k, n).start()
 
+    left_factors(limits_ref, energy_ref, left_ref, split_ref)
+
     def prepare(k):
         for n in range(kinds * halves):
             fetch(k, n).wait()
-            high, low = split_high_low(buffer_ref[k, n])
-            parts_ref[0, k, n * times : (n + 1) * times, :] = high
-            parts_ref[1, k, n * times : (n + 1) * times, :] = low
-
-    integral_into(limits_ref, energy_ref, parts_ref, out_refs, split_ref, prepare)
+            for m, place in enumerate(PLACES):
+                owner = (limits_ref[0] + place) % len(PLACES)
+                block = buffer_ref[k, n, :, pl.ds(pl.multiple_of(owner * LANES, LANES), LANES)]
+                high, low = split_high_low(block)
+                parts_ref[0, k, n * times : (n + 1) * times, m * LANES : (m + 1) * LANES] = high
+                parts_ref[1, k, n * times : (n + 1) * times, m * LANES : (m + 1) * LANES] = low
+
+    products_into(left_ref, parts_ref, out_refs, 0, prepare)
 
 
 def slope_of(parts, state, band_ref):
@@ -194,20 +213,20 @@
     )
 
 
-def predict_kernel(own_ref, one_ref, two_ref, three_ref, state_ref, band_ref, out_ref, base_ref):
+def predict_kernel(first_ref, second_ref, third_ref, own_ref, state_ref, band_ref, out_ref, base_ref):
     state = state_ref[...]
-    slope = slope_of((own_ref, one_ref, two_ref, three_ref), state, band_ref)
+    slope = slope_of((first_ref, second_ref, third_ref, own_ref), state, band_ref)
     out_ref[...] = state + TIME_STEP * slope
     base_ref[...] = state + (0.5 * TIME_STEP) * slope
 
 
-def correct_kernel(own_ref, one_ref, two_ref, three_ref, state_ref, band_ref, base_ref, out_ref):
-    slope = slope_of((own_ref, one_ref, two_ref, three_ref), state_ref[...], band_ref)
+def correct_kernel(first_ref, second_ref, third_ref, own_ref, state_ref, band_ref, base_ref, out_ref):
+    slope = slope_of((first_ref, second_ref, third_ref, own_ref), state_ref[...], band_ref)
     out_ref[...] = base_ref[...] + (0.5 * TIME_STEP) * slope
 
 
-def last_kernel(own_ref, one_ref, two_ref, three_ref, state_ref, band_ref, base_ref, out_ref, split_ref):
-    slope = slope_of((own_ref, one_ref, two_ref, three_ref), state_ref[...], band_ref)
+def last_kernel(first_ref, second_ref, third_ref, own_ref, state_ref, band_ref, base_ref, out_ref, split_ref):
+    slope = slope_of((first_ref, second_ref, third_ref, own_ref), state_ref[...], band_ref)
     value = base_ref[...] + (0.5 * TIME_STEP) * slope
     block = band_ref.shape[0]
     parts = swap_groups([value[q * block : (q + 1) * block] for q in range(4)])
@@ -228,7 +247,8 @@
         high = lax.reduce_precision(table, 8, 7)
         parts.append((high.astype(BF16), (table - high).astype(BF16)))
     (cos_high, cos_low), (sin_high, sin_low) = parts
-    return jnp.concatenate([cos_high, sin_high, cos_low, sin_low], axis=1)
+    high = jnp.concatenate([cos_high, sin_high], axis=1)
+    return jnp.concatenate([high, jnp.concatenate([cos_low, sin_low], axis=1)], axis=0)
 
 
 def band_rows(own_map, first_times, offset):
@@ -260,15 +280,34 @@
     site = resident(site_kernel, [packed_shape], [vmem] * 2, "site")
     tm_size = lax.axis_size("tm")
     split_scratch = vmem((4, block, LANES), F32)
-    integral = resident(
-        integral_kernel, [packed_shape] * tm_size, [pltpu.SMEM, vmem, vmem], "integral", [split_scratch]
+    left_shape = jax.ShapeDtypeStruct((own, 4 * row_count, 4 * LANES), BF16)
+    far_integral = resident(
+        far_integral_kernel,
+        [packed_shape] * FAR + [left_shape],
+        [pltpu.SMEM, vmem, vmem],
+        "far_integral",
+        [split_scratch],
+    )
+    near = tm_size - FAR
+    near_cost = pl.CostEstimate(
+        flops=2 * own * 6 * row_count * stored * near * LANES,
+        transcendentals=0,
+        bytes_accessed=2 * 2 * own * stored * near * LANES,
+    )
+    near_integral = resident(
+        near_integral_kernel, [packed_shape] * near, [vmem, vmem], "near_integral", cost=near_cost
     )
     first_integral = resident(
         first_integral_kernel,
         [packed_shape] * tm_size + [parts_shape],
         [pltpu.SMEM, vmem, pltpu.HBM],
         "first_integral",
-        [split_scratch, vmem((own, 6, time_count, hist), F32), pltpu.SemaphoreType.DMA((own, 6))],
+        [
+            vmem(left_shape.shape, BF16),
+            split_scratch,
+            vmem((own, 6, time_count, hist), F32),
+            pltpu.SemaphoreType.DMA((own, 6)),
+        ],
         9 << 20,
     )
     predict = resident(predict_kernel, [packed_shape] * 2, [vmem] * 6, "predict")
@@ -282,9 +321,11 @@
         return lax.all_to_all(value, "mom", 0, 0, tiled=True)
 
     def exchange(partial):
-        hops = {n: [(t, (t + n) % tm_size) for t in range(tm_size)] for n in (2, 1, 3)}
-        parts = {n: lax.ppermute(partial[n], "tm", hop) for n, hop in hops.items()}
-        return partial[0], parts[2], parts[1], parts[3]
+        moved = [
+            lax.ppermute(value, "tm", [(t, (t + place) % tm_size) for t in range(tm_size)])
+            for value, place in zip(partial[:-1], PLACES[:-1], strict=True)
+        ]
+        return *moved, partial[-1]
 
     def energy_of(arrived):
         (energy,) = site(table, arrived)
@@ -295,7 +336,8 @@
     *partial, stored_parts = first_integral(limits, energy_of(first), history)
 
     def parts_of(estimate):
-        return exchange(integral(limits, energy_of(turned(estimate)), stored_parts))
+        *far, left = far_integral(limits, energy_of(turned(estimate)), stored_parts)
+        return exchange(far + list(near_integral(left, stored_parts)))
 
     for time_step in range(2):
         parts = exchange(partial) if time_step == 0 else parts_of(state)

time: 275 us -> 272 us (0.989)
  waiting for transfers between devices: 37.1 us -> 32.3 us
    ppermute x18, waiting for transfers between devices: 30.8 us -> 25.9 us  [exchange(): lax.ppermute(value, 'tm', [(t, (t + place) % tm_size) for t in range(tm_s...]
    pallas_call x19 -> x24, Pallas kernels: 24.3 us -> 25 us  [apply(): return call(*placed)]
  transfers between devices with their start and end apart: 19 -> 19, of which waited for: 13 -> 13; matrix products, arithmetic and copies ran while one was open for 1% -> 1% of each run, Pallas kernels for 0% -> 1%
where the time goes in v3:
time: 272 us
  blocking collectives  168 us (62%)
  starting transfers between devices  40 us (15%)
  waiting for transfers between devices  32.3 us (12%)
  Pallas kernels  25 us (9%)
  other arithmetic  3.16 us (1%)
    all_to_all x11, blocking collectives, turned(): return lax.all_to_all(value, 'mom', 0, 0, tiled=True)  168 us
    ppermute x18, starting transfers between devices, exchange(): lax.ppermute(value, 'tm', [(t, (t + place) % tm_size) for t in range(tm_s...  27 us
    ppermute x18, waiting for transfers between devices, exchange(): lax.ppermute(value, 'tm', [(t, (t + place) % tm_size) for t in range(tm_s...  25.9 us
    pallas_call x24, Pallas kernels, apply(): return call(*placed)  25 us
    all_to_all x1, starting transfers between devices, turned(): return lax.all_to_all(value, 'mom', 0, 0, tiled=True)  13 us
    all_to_all x1, waiting for transfers between devices, turned(): return lax.all_to_all(value, 'mom', 0, 0, tiled=True)  6.35 us
  transfers between devices with their start and end apart: 19, of which 13 were waited for; matrix products, arithmetic and copies ran while one was open for 1% of the time, Pallas kernels for 1%

profile of v3, /device:TPU:1, one launch (start us, length us, event | category | flops | bytes accessed | tf_op | source)
XLA Modules:
  0.0 271.6 jit_solution(18114837733371863565)
XLA Ops:
  1.7 13.0 %all-to-all-start = ((f32[64,4,128]{2,1,0:T(4,128)}), f32[64,4,128]{2,1,0:T(4,128)S(1)}, u32[]{:S(2)}, u32[]{:S(2)}) async-start(f32[64,4,128]{2,1,0:T(4,128)} %bitcast), calls=%async_computation | async-start | bytes 262144 | tf_op jit(solution)/shard_map/all_to_all | solution.py:321
  19.5 6.3 %all-to-all-done = f32[64,4,128]{2,1,0:T(4,128)S(1)} async-done(((f32[64,4,128]{2,1,0:T(4,128)}), f32[64,4,128]{2,1,0:T(4,128)S(1)}, u32[]{:S(2)}, u32[]{:S(2)}) %all-to-all-start) | async-done | bytes 131104 | tf_op jit(solution)/shard_map/all_to_all | solution.py:321
  27.1 14.9 %all_to_all.133 = f32[64,4,128]{2,1,0:T(4,128)S(1)} all-to-all(f32[64,4,128]{2,1,0:T(4,128)S(1)} %bitcast.37), channel_id=1, replica_groups=mesh['mom'=64,'tm'=4] {'mom'}, dimensions={0} | all-to-all | bytes 262144 | tf_op jit(solution)/shard_map/all_to_all | solution.py:321
  42.0 4.5 %first_integral.1 = (f32[256,128]{1,0:T(8,128)S(1)}, f32[256,128]{1,0:T(8,128)S(1)}, f32[256,128]{1,0:T(8,128)S(1)}, f32[256,128]{1,0:T(8,128)S(1)}, bf16[2,4,768,512]{3,2,1,0:T(8,128)(2,1)S(1)}) custom-call(s32[2]{0:T(128)S(1)} %pad_add_fusion.limits_ref, f32[256,128]{1,0:T(8,128)S(1)} %bitcast.29, f32[3,2,4,128,512]{4,3,2,1,0:T(8,128)} %stored_ref.1), custom_call_target="tpu_custom_call" | custom-call | tf_op jit(solution)/shard_map/first_integral/pallas_call | solution.py:66
  46.6 3.0 %collective-permute-start = (f32[256,128]{1,0:T(8,128)S(1)}, f32[256,128]{1,0:T(8,128)S(1)}, u32[]{:S(2)}, u32[]{:S(2)}) collective-permute-start(f32[256,128]{1,0:T(8,128)S(1)} %get-tuple-element.46), channel_id=1, source_target_pairs={{0,2},{1,3},{2,0},{3,1},{4,6},{5,7},{6,4},{7,5},{8,10},{9,11},{10,... | collective-permute-start | bytes 393224 | tf_op jit(solution)/shard_map/ppermute | solution.py:325
  50.0 2.3 collective-permute-start.2
  52.9 3.3 %collective-permute-done.1.second_ref = f32[256,128]{1,0:T(8,128)S(1)} collective-permute-done((f32[256,128]{1,0:T(8,128)S(1)}, f32[256,128]{1,0:T(8,128)S(1)}, u32[]{:S(2)}, u32[]{:S(2)}) %collective-permute-start.1) | collective-permute-done | bytes 131104 | tf_op jit(solution)/shard_map/ppermute | solution.py:325
  57.4 15.6 %all_to_all.134 = f32[64,4,128]{2,1,0:T(4,128)S(1)} all-to-all(f32[64,4,128]{2,1,0:T(4,128)S(1)} %bitcast.47), channel_id=1, replica_groups=mesh['mom'=64,'tm'=4] {'mom'}, dimensions={0} | all-to-all | bytes 262144 | tf_op jit(solution)/shard_map/all_to_all | solution.py:321
  74.0 14.9 %all_to_all.135 = f32[64,4,128]{2,1,0:T(4,128)S(1)} all-to-all(f32[64,4,128]{2,1,0:T(4,128)S(1)} %bitcast.38), channel_id=1, replica_groups=mesh['mom'=64,'tm'=4] {'mom'}, dimensions={0} | all-to-all | bytes 262144 | tf_op jit(solution)/shard_map/all_to_all | solution.py:321
  90.1 1.9 collective-permute-start.3
  96.4 2.8 %collective-permute-done.4.second_ref = f32[256,128]{1,0:T(8,128)S(1)} collective-permute-done((f32[256,128]{1,0:T(8,128)S(1)}, f32[256,128]{1,0:T(8,128)S(1)}, u32[]{:S(2)}, u32[]{:S(2)}) %collective-permute-start.4) | collective-permute-done | bytes 131104 | tf_op jit(solution)/shard_map/ppermute | solution.py:325
  99.5 16.1 %all_to_all.136 = f32[64,4,128]{2,1,0:T(4,128)S(1)} all-to-all(f32[64,4,128]{2,1,0:T(4,128)S(1)} %bitcast.28), channel_id=1, replica_groups=mesh['mom'=64,'tm'=4] {'mom'}, dimensions={0} | all-to-all | bytes 262144 | tf_op jit(solution)/shard_map/all_to_all | solution.py:321
  116.6 14.9 %all_to_all.137 = f32[64,4,128]{2,1,0:T(4,128)S(1)} all-to-all(f32[64,4,128]{2,1,0:T(4,128)S(1)} %bitcast.39), channel_id=1, replica_groups=mesh['mom'=64,'tm'=4] {'mom'}, dimensions={0} | all-to-all | bytes 262144 | tf_op jit(solution)/shard_map/all_to_all | solution.py:321
  139.0 3.1 %collective-permute-done.7.second_ref = f32[256,128]{1,0:T(8,128)S(1)} collective-permute-done((f32[256,128]{1,0:T(8,128)S(1)}, f32[256,128]{1,0:T(8,128)S(1)}, u32[]{:S(2)}, u32[]{:S(2)}) %collective-permute-start.7) | collective-permute-done | bytes 131104 | tf_op jit(solution)/shard_map/ppermute | solution.py:325
  142.4 15.5 %all_to_all.138 = f32[64,4,128]{2,1,0:T(4,128)S(1)} all-to-all(f32[64,4,128]{2,1,0:T(4,128)S(1)} %bitcast.26), channel_id=1, replica_groups=mesh['mom'=64,'tm'=4] {'mom'}, dimensions={0} | all-to-all | bytes 262144 | tf_op jit(solution)/shard_map/all_to_all | solution.py:321
  158.9 14.9 %all_to_all.139 = f32[64,4,128]{2,1,0:T(4,128)S(1)} all-to-all(f32[64,4,128]{2,1,0:T(4,128)S(1)} %bitcast.40), channel_id=1, replica_groups=mesh['mom'=64,'tm'=4] {'mom'}, dimensions={0} | all-to-all | bytes 262144 | tf_op jit(solution)/shard_map/all_to_all | solution.py:321
  181.3 3.1 %collective-permute-done.10.second_ref = f32[256,128]{1,0:T(8,128)S(1)} collective-permute-done((f32[256,128]{1,0:T(8,128)S(1)}, f32[256,128]{1,0:T(8,128)S(1)}, u32[]{:S(2)}, u32[]{:S(2)}) %collective-permute-start.10) | collective-permute-done | bytes 131104 | tf_op jit(solution)/shard_map/ppermute | solution.py:325
  184.6 15.7 %all_to_all.140 = f32[64,4,128]{2,1,0:T(4,128)S(1)} all-to-all(f32[64,4,128]{2,1,0:T(4,128)S(1)} %bitcast.48), channel_id=1, replica_groups=mesh['mom'=64,'tm'=4] {'mom'}, dimensions={0} | all-to-all | bytes 262144 | tf_op jit(solution)/shard_map/all_to_all | solution.py:321
  201.4 14.9 %all_to_all.141 = f32[64,4,128]{2,1,0:T(4,128)S(1)} all-to-all(f32[64,4,128]{2,1,0:T(4,128)S(1)} %bitcast.41), channel_id=1, replica_groups=mesh['mom'=64,'tm'=4] {'mom'}, dimensions={0} | all-to-all | bytes 262144 | tf_op jit(solution)/shard_map/all_to_all | solution.py:321
  223.8 3.1 %collective-permute-done.13.second_ref = f32[256,128]{1,0:T(8,128)S(1)} collective-permute-done((f32[256,128]{1,0:T(8,128)S(1)}, f32[256,128]{1,0:T(8,128)S(1)}, u32[]{:S(2)}, u32[]{:S(2)}) %collective-permute-start.13) | collective-permute-done | bytes 131104 | tf_op jit(solution)/shard_map/ppermute | solution.py:325
  227.2 15.5 %all_to_all.142 = f32[64,4,128]{2,1,0:T(4,128)S(1)} all-to-all(f32[64,4,128]{2,1,0:T(4,128)S(1)} %bitcast.27), channel_id=1, replica_groups=mesh['mom'=64,'tm'=4] {'mom'}, dimensions={0} | all-to-all | bytes 262144 | tf_op jit(solution)/shard_map/all_to_all | solution.py:321
  243.7 14.9 %all_to_all.143 = f32[64,4,128]{2,1,0:T(4,128)S(1)} all-to-all(f32[64,4,128]{2,1,0:T(4,128)S(1)} %bitcast.36), channel_id=1, replica_groups=mesh['mom'=64,'tm'=4] {'mom'}, dimensions={0} | all-to-all | bytes 262144 | tf_op jit(solution)/shard_map/all_to_all | solution.py:321
  264.4 2.3 collective-permute-done.16.second_ref
  266.7 3.8 %collective-permute-done.15.first_ref = f32[256,128]{1,0:T(8,128)S(1)} collective-permute-done((f32[256,128]{1,0:T(8,128)S(1)}, f32[256,128]{1,0:T(8,128)S(1)}, u32[]{:S(2)}, u32[]{:S(2)}) %collective-permute-start.15) | collective-permute-done | bytes 131104 | tf_op jit(solution)/shard_map/ppermute | solution.py:325
  (67 shorter events, 49.8 us)
Async XLA Ops:
  0.0 0.9 copy-start
  1.7 24.1 %all-to-all-start = ((f32[64,4,128]{2,1,0:T(4,128)}), f32[64,4,128]{2,1,0:T(4,128)S(1)}, u32[]{:S(2)}, u32[]{:S(2)}) async-start(f32[64,4,128]{2,1,0:T(4,128)} %bitcast), calls=%async_computation | async-start | bytes 262144 | tf_op jit(solution)/shard_map/all_to_all | solution.py:321
  46.6 6.3 %collective-permute-start = (f32[256,128]{1,0:T(8,128)S(1)}, f32[256,128]{1,0:T(8,128)S(1)}, u32[]{:S(2)}, u32[]{:S(2)}) collective-permute-start(f32[256,128]{1,0:T(8,128)S(1)} %get-tuple-element.46), channel_id=1, source_target_pairs={{0,2},{1,3},{2,0},{3,1},{4,6},{5,7},{6,4},{7,5},{8,10},{9,11},{10,... | collective-permute-start | bytes 393224 | tf_op jit(solution)/shard_map/ppermute | solution.py:325
  49.6 6.6 %collective-permute-start.1 = (f32[256,128]{1,0:T(8,128)S(1)}, f32[256,128]{1,0:T(8,128)S(1)}, u32[]{:S(2)}, u32[]{:S(2)}) collective-permute-start(f32[256,128]{1,0:T(8,128)S(1)} %get-tuple-element.47), channel_id=1, source_target_pairs={{0,1},{1,2},{2,3},{3,0},{4,5},{5,6},{6,7},{7,4},{8,9},{9,10},{10,1... | collective-permute-start | bytes 393224 | tf_op jit(solution)/shard_map/ppermute | solution.py:325
  50.0 6.2 %collective-permute-start.2 = (f32[256,128]{1,0:T(8,128)S(1)}, f32[256,128]{1,0:T(8,128)S(1)}, u32[]{:S(2)}, u32[]{:S(2)}) collective-permute-start(f32[256,128]{1,0:T(8,128)S(1)} %get-tuple-element.48), channel_id=1, source_target_pairs={{0,3},{1,0},{2,1},{3,2},{4,7},{5,4},{6,5},{7,6},{8,11},{9,8},{10,9... | collective-permute-start | bytes 393224 | tf_op jit(solution)/shard_map/ppermute | solution.py:325
  90.1 6.3 %collective-permute-start.3 = (f32[256,128]{1,0:T(8,128)S(1)}, f32[256,128]{1,0:T(8,128)S(1)}, u32[]{:S(2)}, u32[]{:S(2)}) collective-permute-start(f32[256,128]{1,0:T(8,128)S(1)} %get-tuple-element.53), channel_id=1, source_target_pairs={{0,2},{1,3},{2,0},{3,1},{4,6},{5,7},{6,4},{7,5},{8,10},{9,11},{10,... | collective-permute-start | bytes 393224 | tf_op jit(solution)/shard_map/ppermute | solution.py:325
  92.9 6.3 %collective-permute-start.4 = (f32[256,128]{1,0:T(8,128)S(1)}, f32[256,128]{1,0:T(8,128)S(1)}, u32[]{:S(2)}, u32[]{:S(2)}) collective-permute-start(f32[256,128]{1,0:T(8,128)S(1)} %get-tuple-element.55), channel_id=1, source_target_pairs={{0,1},{1,2},{2,3},{3,0},{4,5},{5,6},{6,7},{7,4},{8,9},{9,10},{10,1... | collective-permute-start | bytes 393224 | tf_op jit(solution)/shard_map/ppermute | solution.py:325
  94.5 4.7 %collective-permute-start.5 = (f32[256,128]{1,0:T(8,128)S(1)}, f32[256,128]{1,0:T(8,128)S(1)}, u32[]{:S(2)}, u32[]{:S(2)}) collective-permute-start(f32[256,128]{1,0:T(8,128)S(1)} %get-tuple-element.56), channel_id=1, source_target_pairs={{0,3},{1,0},{2,1},{3,2},{4,7},{5,4},{6,5},{7,6},{8,11},{9,8},{10,9... | collective-permute-start | bytes 393224 | tf_op jit(solution)/shard_map/ppermute | solution.py:325
  132.8 6.3 %collective-permute-start.6 = (f32[256,128]{1,0:T(8,128)S(1)}, f32[256,128]{1,0:T(8,128)S(1)}, u32[]{:S(2)}, u32[]{:S(2)}) collective-permute-start(f32[256,128]{1,0:T(8,128)S(1)} %get-tuple-element.60), channel_id=1, source_target_pairs={{0,2},{1,3},{2,0},{3,1},{4,6},{5,7},{6,4},{7,5},{8,10},{9,11},{10,... | collective-permute-start | bytes 393224 | tf_op jit(solution)/shard_map/ppermute | solution.py:325
  135.3 6.9 %collective-permute-start.7 = (f32[256,128]{1,0:T(8,128)S(1)}, f32[256,128]{1,0:T(8,128)S(1)}, u32[]{:S(2)}, u32[]{:S(2)}) collective-permute-start(f32[256,128]{1,0:T(8,128)S(1)} %get-tuple-element.62), channel_id=1, source_target_pairs={{0,1},{1,2},{2,3},{3,0},{4,5},{5,6},{6,7},{7,4},{8,9},{9,10},{10,1... | collective-permute-start | bytes 393224 | tf_op jit(solution)/shard_map/ppermute | solution.py:325
  136.8 5.3 %collective-permute-start.8 = (f32[256,128]{1,0:T(8,128)S(1)}, f32[256,128]{1,0:T(8,128)S(1)}, u32[]{:S(2)}, u32[]{:S(2)}) collective-permute-start(f32[256,128]{1,0:T(8,128)S(1)} %get-tuple-element.63), channel_id=1, source_target_pairs={{0,3},{1,0},{2,1},{3,2},{4,7},{5,4},{6,5},{7,6},{8,11},{9,8},{10,9... | collective-permute-start | bytes 393224 | tf_op jit(solution)/shard_map/ppermute | solution.py:325
  175.0 6.3 %collective-permute-start.9 = (f32[256,128]{1,0:T(8,128)S(1)}, f32[256,128]{1,0:T(8,128)S(1)}, u32[]{:S(2)}, u32[]{:S(2)}) collective-permute-start(f32[256,128]{1,0:T(8,128)S(1)} %get-tuple-element.65), channel_id=1, source_target_pairs={{0,2},{1,3},{2,0},{3,1},{4,6},{5,7},{6,4},{7,5},{8,10},{9,11},{10,... | collective-permute-start | bytes 393224 | tf_op jit(solution)/shard_map/ppermute | solution.py:325
  177.5 6.9 %collective-permute-start.10 = (f32[256,128]{1,0:T(8,128)S(1)}, f32[256,128]{1,0:T(8,128)S(1)}, u32[]{:S(2)}, u32[]{:S(2)}) collective-permute-start(f32[256,128]{1,0:T(8,128)S(1)} %get-tuple-element.67), channel_id=1, source_target_pairs={{0,1},{1,2},{2,3},{3,0},{4,5},{5,6},{6,7},{7,4},{8,9},{9,10},{10,1... | collective-permute-start | bytes 393224 | tf_op jit(solution)/shard_map/ppermute | solution.py:325
  179.1 5.3 %collective-permute-start.11 = (f32[256,128]{1,0:T(8,128)S(1)}, f32[256,128]{1,0:T(8,128)S(1)}, u32[]{:S(2)}, u32[]{:S(2)}) collective-permute-start(f32[256,128]{1,0:T(8,128)S(1)} %get-tuple-element.68), channel_id=1, source_target_pairs={{0,3},{1,0},{2,1},{3,2},{4,7},{5,4},{6,5},{7,6},{8,11},{9,8},{10,9... | collective-permute-start | bytes 393224 | tf_op jit(solution)/shard_map/ppermute | solution.py:325
  217.6 6.3 %collective-permute-start.12 = (f32[256,128]{1,0:T(8,128)S(1)}, f32[256,128]{1,0:T(8,128)S(1)}, u32[]{:S(2)}, u32[]{:S(2)}) collective-permute-start(f32[256,128]{1,0:T(8,128)S(1)} %get-tuple-element.71), channel_id=1, source_target_pairs={{0,2},{1,3},{2,0},{3,1},{4,6},{5,7},{6,4},{7,5},{8,10},{9,11},{10,... | collective-permute-start | bytes 393224 | tf_op jit(solution)/shard_map/ppermute | solution.py:325
  220.1 6.9 %collective-permute-start.13 = (f32[256,128]{1,0:T(8,128)S(1)}, f32[256,128]{1,0:T(8,128)S(1)}, u32[]{:S(2)}, u32[]{:S(2)}) collective-permute-start(f32[256,128]{1,0:T(8,128)S(1)} %get-tuple-element.73), channel_id=1, source_target_pairs={{0,1},{1,2},{2,3},{3,0},{4,5},{5,6},{6,7},{7,4},{8,9},{9,10},{10,1... | collective-permute-start | bytes 393224 | tf_op jit(solution)/shard_map/ppermute | solution.py:325
  221.6 5.3 %collective-permute-start.14 = (f32[256,128]{1,0:T(8,128)S(1)}, f32[256,128]{1,0:T(8,128)S(1)}, u32[]{:S(2)}, u32[]{:S(2)}) collective-permute-start(f32[256,128]{1,0:T(8,128)S(1)} %get-tuple-element.74), channel_id=1, source_target_pairs={{0,3},{1,0},{2,1},{3,2},{4,7},{5,4},{6,5},{7,6},{8,11},{9,8},{10,9... | collective-permute-start | bytes 393224 | tf_op jit(solution)/shard_map/ppermute | solution.py:325
  260.7 6.0 %collective-permute-start.16 = (f32[256,128]{1,0:T(8,128)S(1)}, f32[256,128]{1,0:T(8,128)S(1)}, u32[]{:S(2)}, u32[]{:S(2)}) collective-permute-start(f32[256,128]{1,0:T(8,128)S(1)} %get-tuple-element.80), channel_id=1, source_target_pairs={{0,1},{1,2},{2,3},{3,0},{4,5},{5,6},{6,7},{7,4},{8,9},{9,10},{10,1... | collective-permute-start | bytes 393224 | tf_op jit(solution)/shard_map/ppermute | solution.py:325
  261.6 5.1 %collective-permute-start.17 = (f32[256,128]{1,0:T(8,128)S(1)}, f32[256,128]{1,0:T(8,128)S(1)}, u32[]{:S(2)}, u32[]{:S(2)}) collective-permute-start(f32[256,128]{1,0:T(8,128)S(1)} %get-tuple-element.81), channel_id=1, source_target_pairs={{0,3},{1,0},{2,1},{3,2},{4,7},{5,4},{6,5},{7,6},{8,11},{9,8},{10,9... | collective-permute-start | bytes 393224 | tf_op jit(solution)/shard_map/ppermute | solution.py:325
  263.5 7.0 %collective-permute-start.15 = (f32[256,128]{1,0:T(8,128)S(1)}, f32[256,128]{1,0:T(8,128)S(1)}, u32[]{:S(2)}, u32[]{:S(2)}) collective-permute-start(f32[256,128]{1,0:T(8,128)S(1)} %get-tuple-element.78), channel_id=1, source_target_pairs={{0,2},{1,3},{2,0},{3,1},{4,6},{5,7},{6,4},{7,5},{8,10},{9,11},{10,... | collective-permute-start | bytes 393224 | tf_op jit(solution)/shard_map/ppermute | solution.py:325

commit v4 on v3

--- a/solution.py
+++ b/solution.py
@@ -68,13 +68,15 @@
     return apply
 
 
-def pack_kernel(rows_ref, out_ref):
+def pack_kernel(rows_ref, out_ref, kept_ref):
     row_count = rows_ref.shape[2]
     own = rows_ref.shape[1]
     for k in range(own):
         packed = swap_groups([rows_ref[c, k] for c in range(4)])
         for q in range(4):
-            out_ref[pl.ds(q * own * row_count + k, row_count, stride=own), :] = packed[q]
+            target = pl.ds(q * own * row_count + k, row_count, stride=own)
+            out_ref[target, :] = packed[q]
+            kept_ref[target, :] = packed[q]
 
 
 def transform(table_ref, value, turned):
@@ -139,7 +141,7 @@
             left_ref[k, 2 * rows :, columns] = low
 
 
-def products_into(left_ref, parts_ref, out_refs, first, prepare=None):
+def products_into(left_ref, parts_ref, out_refs, first, together, prepare=None):
     own = left_ref.shape[0]
     rows = left_ref.shape[1] // 4
     block = own * rows
@@ -163,17 +165,25 @@
                 out_ref[pl.ds(c * block + k, rows, stride=own), :] = value[:, n * LANES : (n + 1) * LANES]
         return carry
 
-    lax.fori_loop(0, own // 2, lambda pair, carry: each(2 * pair + 1, each(2 * pair, carry)), 0)
+    def several(step, carry):
+        for n in range(together):
+            carry = each(step * together + n, carry)
+        return carry
+
+    if together == own:
+        several(0, 0)
+    else:
+        lax.fori_loop(0, own // together, several, 0)
 
 
 def far_integral_kernel(limits_ref, energy_ref, parts_ref, *refs):
     *out_refs, left_ref, split_ref = refs
     left_factors(limits_ref, energy_ref, left_ref, split_ref)
-    products_into(left_ref, parts_ref, out_refs, 0)
+    products_into(left_ref, parts_ref, out_refs, 0, 4)
 
 
 def near_integral_kernel(left_ref, parts_ref, *out_refs):
-    products_into(left_ref, parts_ref, out_refs, len(PLACES) - len(out_refs))
+    products_into(left_ref, parts_ref, out_refs, len(PLACES) - len(out_refs), 1)
 
 
 def first_integral_kernel(limits_ref, energy_ref, stored_ref, *refs):
@@ -200,7 +210,7 @@
                 parts_ref[0, k, n * times : (n + 1) * times, m * LANES : (m + 1) * LANES] = high
                 parts_ref[1, k, n * times : (n + 1) * times, m * LANES : (m + 1) * LANES] = low
 
-    products_into(left_ref, parts_ref, out_refs, 0, prepare)
+    products_into(left_ref, parts_ref, out_refs, 0, 1, prepare)
 
 
 def slope_of(parts, state, band_ref):
@@ -274,7 +284,7 @@
     limits = jnp.stack([lax.axis_index("tm"), history_len[0]])
 
     vmem = pltpu.VMEM
-    pack = resident(pack_kernel, [packed_shape], [vmem], "pack")
+    pack = resident(pack_kernel, [packed_shape] * 2, [vmem], "pack")
     stored = 6 * time_count
     parts_shape = jax.ShapeDtypeStruct((2, own, stored, hist), BF16)
     site = resident(site_kernel, [packed_shape], [vmem] * 2, "site")
@@ -315,7 +325,7 @@
     last = resident(
         last_kernel, [jax.ShapeDtypeStruct(new_rows.shape, F32)], [vmem] * 7, "last", [split_scratch]
     )
-    (state,) = pack(new_rows)
+    sent, state = pack(new_rows)
 
     def turned(value):
         return lax.all_to_all(value, "mom", 0, 0, tiled=True)
@@ -331,7 +341,7 @@
         (energy,) = site(table, arrived)
         return turned(energy)
 
-    first = turned(state)
+    first = turned(sent)
     first, limits, bands = lax.optimization_barrier((first, limits, bands))
     *partial, stored_parts = first_integral(limits, energy_of(first), history)
 

time: 272 us -> 270 us (level)
  transfers between devices with their start and end apart: 19 -> 19, of which waited for: 13 -> 13; matrix products, arithmetic and copies ran while one was open for 1% -> 1% of each run, Pallas kernels for 1% -> 2%
where the time goes in v4:
time: 270 us
  blocking collectives  169 us (63%)
  starting transfers between devices  39.9 us (15%)
  waiting for transfers between devices  30.2 us (11%)
  Pallas kernels  24.3 us (9%)
  other arithmetic  3.16 us (1%)
    all_to_all x11, blocking collectives, turned(): return lax.all_to_all(value, 'mom', 0, 0, tiled=True)  169 us
    ppermute x18, starting transfers between devices, exchange(): lax.ppermute(value, 'tm', [(t, (t + place) % tm_size) for t in range(tm_s...  26.9 us
    pallas_call x24, Pallas kernels, apply(): return call(*placed)  24.3 us
    ppermute x18, waiting for transfers between devices, exchange(): lax.ppermute(value, 'tm', [(t, (t + place) % tm_size) for t in range(tm_s...  23.9 us
    all_to_all x1, starting transfers between devices, turned(): return lax.all_to_all(value, 'mom', 0, 0, tiled=True)  13 us
    all_to_all x1, waiting for transfers between devices, turned(): return lax.all_to_all(value, 'mom', 0, 0, tiled=True)  6.35 us
  transfers between devices with their start and end apart: 19, of which 13 were waited for; matrix products, arithmetic and copies ran while one was open for 1% of the time, Pallas kernels for 2%

profile of v4, /device:TPU:1, one launch (start us, length us, event | category | flops | bytes accessed | tf_op | source)
XLA Modules:
  0.0 269.7 jit_solution(8359684453279148149)
XLA Ops:
  1.7 13.0 %all-to-all-start = ((f32[64,4,128]{2,1,0:T(4,128)}), f32[64,4,128]{2,1,0:T(4,128)S(1)}, u32[]{:S(2)}, u32[]{:S(2)}) async-start(f32[64,4,128]{2,1,0:T(4,128)} %bitcast), calls=%async_computation | async-start | bytes 262144 | tf_op jit(solution)/shard_map/all_to_all | solution.py:331
  19.5 6.3 %all-to-all-done = f32[64,4,128]{2,1,0:T(4,128)S(1)} async-done(((f32[64,4,128]{2,1,0:T(4,128)}), f32[64,4,128]{2,1,0:T(4,128)S(1)}, u32[]{:S(2)}, u32[]{:S(2)}) %all-to-all-start) | async-done | bytes 131104 | tf_op jit(solution)/shard_map/all_to_all | solution.py:331
  27.1 14.9 %all_to_all.133 = f32[64,4,128]{2,1,0:T(4,128)S(1)} all-to-all(f32[64,4,128]{2,1,0:T(4,128)S(1)} %bitcast.37), channel_id=1, replica_groups=mesh['mom'=64,'tm'=4] {'mom'}, dimensions={0} | all-to-all | bytes 262144 | tf_op jit(solution)/shard_map/all_to_all | solution.py:331
  42.0 4.5 %first_integral.1 = (f32[256,128]{1,0:T(8,128)S(1)}, f32[256,128]{1,0:T(8,128)S(1)}, f32[256,128]{1,0:T(8,128)S(1)}, f32[256,128]{1,0:T(8,128)S(1)}, bf16[2,4,768,512]{3,2,1,0:T(8,128)(2,1)S(1)}) custom-call(s32[2]{0:T(128)S(1)} %pad_add_fusion.limits_ref, f32[256,128]{1,0:T(8,128)S(1)} %bitcast.29, f32[3,2,4,128,512]{4,3,2,1,0:T(8,128)} %stored_ref.1), custom_call_target="tpu_custom_call" | custom-call | tf_op jit(solution)/shard_map/first_integral/pallas_call | solution.py:66
  46.6 3.0 %collective-permute-start = (f32[256,128]{1,0:T(8,128)S(1)}, f32[256,128]{1,0:T(8,128)S(1)}, u32[]{:S(2)}, u32[]{:S(2)}) collective-permute-start(f32[256,128]{1,0:T(8,128)S(1)} %get-tuple-element.49), channel_id=1, source_target_pairs={{0,2},{1,3},{2,0},{3,1},{4,6},{5,7},{6,4},{7,5},{8,10},{9,11},{10,... | collective-permute-start | bytes 393224 | tf_op jit(solution)/shard_map/ppermute | solution.py:335
  50.0 2.3 collective-permute-start.2
  52.9 3.3 %collective-permute-done.1.second_ref = f32[256,128]{1,0:T(8,128)S(1)} collective-permute-done((f32[256,128]{1,0:T(8,128)S(1)}, f32[256,128]{1,0:T(8,128)S(1)}, u32[]{:S(2)}, u32[]{:S(2)}) %collective-permute-start.1) | collective-permute-done | bytes 131104 | tf_op jit(solution)/shard_map/ppermute | solution.py:335
  56.4 15.6 %all_to_all.134 = f32[64,4,128]{2,1,0:T(4,128)S(1)} all-to-all(f32[64,4,128]{2,1,0:T(4,128)S(1)} %bitcast.47), channel_id=1, replica_groups=mesh['mom'=64,'tm'=4] {'mom'}, dimensions={0} | all-to-all | bytes 262144 | tf_op jit(solution)/shard_map/all_to_all | solution.py:331
  73.1 14.9 %all_to_all.135 = f32[64,4,128]{2,1,0:T(4,128)S(1)} all-to-all(f32[64,4,128]{2,1,0:T(4,128)S(1)} %bitcast.38), channel_id=1, replica_groups=mesh['mom'=64,'tm'=4] {'mom'}, dimensions={0} | all-to-all | bytes 262144 | tf_op jit(solution)/shard_map/all_to_all | solution.py:331
  89.0 1.9 collective-permute-start.3
  95.3 2.6 collective-permute-done.4.second_ref
  98.1 16.3 %all_to_all.136 = f32[64,4,128]{2,1,0:T(4,128)S(1)} all-to-all(f32[64,4,128]{2,1,0:T(4,128)S(1)} %bitcast.28), channel_id=1, replica_groups=mesh['mom'=64,'tm'=4] {'mom'}, dimensions={0} | all-to-all | bytes 262144 | tf_op jit(solution)/shard_map/all_to_all | solution.py:331
  115.5 14.9 %all_to_all.137 = f32[64,4,128]{2,1,0:T(4,128)S(1)} all-to-all(f32[64,4,128]{2,1,0:T(4,128)S(1)} %bitcast.39), channel_id=1, replica_groups=mesh['mom'=64,'tm'=4] {'mom'}, dimensions={0} | all-to-all | bytes 262144 | tf_op jit(solution)/shard_map/all_to_all | solution.py:331
  137.8 2.8 %collective-permute-done.7.second_ref = f32[256,128]{1,0:T(8,128)S(1)} collective-permute-done((f32[256,128]{1,0:T(8,128)S(1)}, f32[256,128]{1,0:T(8,128)S(1)}, u32[]{:S(2)}, u32[]{:S(2)}) %collective-permute-start.7) | collective-permute-done | bytes 131104 | tf_op jit(solution)/shard_map/ppermute | solution.py:335
  140.9 15.7 %all_to_all.138 = f32[64,4,128]{2,1,0:T(4,128)S(1)} all-to-all(f32[64,4,128]{2,1,0:T(4,128)S(1)} %bitcast.26), channel_id=1, replica_groups=mesh['mom'=64,'tm'=4] {'mom'}, dimensions={0} | all-to-all | bytes 262144 | tf_op jit(solution)/shard_map/all_to_all | solution.py:331
  157.6 14.9 %all_to_all.139 = f32[64,4,128]{2,1,0:T(4,128)S(1)} all-to-all(f32[64,4,128]{2,1,0:T(4,128)S(1)} %bitcast.40), channel_id=1, replica_groups=mesh['mom'=64,'tm'=4] {'mom'}, dimensions={0} | all-to-all | bytes 262144 | tf_op jit(solution)/shard_map/all_to_all | solution.py:331
  179.8 2.8 %collective-permute-done.10.second_ref = f32[256,128]{1,0:T(8,128)S(1)} collective-permute-done((f32[256,128]{1,0:T(8,128)S(1)}, f32[256,128]{1,0:T(8,128)S(1)}, u32[]{:S(2)}, u32[]{:S(2)}) %collective-permute-start.10) | collective-permute-done | bytes 131104 | tf_op jit(solution)/shard_map/ppermute | solution.py:335
  182.9 15.7 %all_to_all.140 = f32[64,4,128]{2,1,0:T(4,128)S(1)} all-to-all(f32[64,4,128]{2,1,0:T(4,128)S(1)} %bitcast.48), channel_id=1, replica_groups=mesh['mom'=64,'tm'=4] {'mom'}, dimensions={0} | all-to-all | bytes 262144 | tf_op jit(solution)/shard_map/all_to_all | solution.py:331
  199.7 14.9 %all_to_all.141 = f32[64,4,128]{2,1,0:T(4,128)S(1)} all-to-all(f32[64,4,128]{2,1,0:T(4,128)S(1)} %bitcast.41), channel_id=1, replica_groups=mesh['mom'=64,'tm'=4] {'mom'}, dimensions={0} | all-to-all | bytes 262144 | tf_op jit(solution)/shard_map/all_to_all | solution.py:331
  221.9 2.8 %collective-permute-done.13.second_ref = f32[256,128]{1,0:T(8,128)S(1)} collective-permute-done((f32[256,128]{1,0:T(8,128)S(1)}, f32[256,128]{1,0:T(8,128)S(1)}, u32[]{:S(2)}, u32[]{:S(2)}) %collective-permute-start.13) | collective-permute-done | bytes 131104 | tf_op jit(solution)/shard_map/ppermute | solution.py:335
  225.1 15.8 %all_to_all.142 = f32[64,4,128]{2,1,0:T(4,128)S(1)} all-to-all(f32[64,4,128]{2,1,0:T(4,128)S(1)} %bitcast.27), channel_id=1, replica_groups=mesh['mom'=64,'tm'=4] {'mom'}, dimensions={0} | all-to-all | bytes 262144 | tf_op jit(solution)/shard_map/all_to_all | solution.py:331
  241.9 14.9 %all_to_all.143 = f32[64,4,128]{2,1,0:T(4,128)S(1)} all-to-all(f32[64,4,128]{2,1,0:T(4,128)S(1)} %bitcast.36), channel_id=1, replica_groups=mesh['mom'=64,'tm'=4] {'mom'}, dimensions={0} | all-to-all | bytes 262144 | tf_op jit(solution)/shard_map/all_to_all | solution.py:331
  262.6 2.4 collective-permute-done.16.second_ref
  265.0 3.7 %collective-permute-done.15.first_ref = f32[256,128]{1,0:T(8,128)S(1)} collective-permute-done((f32[256,128]{1,0:T(8,128)S(1)}, f32[256,128]{1,0:T(8,128)S(1)}, u32[]{:S(2)}, u32[]{:S(2)}) %collective-permute-start.15) | collective-permute-done | bytes 131104 | tf_op jit(solution)/shard_map/ppermute | solution.py:335
  (67 shorter events, 48.1 us)
Async XLA Ops:
  0.0 0.9 copy-start
  1.7 24.1 %all-to-all-start = ((f32[64,4,128]{2,1,0:T(4,128)}), f32[64,4,128]{2,1,0:T(4,128)S(1)}, u32[]{:S(2)}, u32[]{:S(2)}) async-start(f32[64,4,128]{2,1,0:T(4,128)} %bitcast), calls=%async_computation | async-start | bytes 262144 | tf_op jit(solution)/shard_map/all_to_all | solution.py:331
  46.6 6.3 %collective-permute-start = (f32[256,128]{1,0:T(8,128)S(1)}, f32[256,128]{1,0:T(8,128)S(1)}, u32[]{:S(2)}, u32[]{:S(2)}) collective-permute-start(f32[256,128]{1,0:T(8,128)S(1)} %get-tuple-element.49), channel_id=1, source_target_pairs={{0,2},{1,3},{2,0},{3,1},{4,6},{5,7},{6,4},{7,5},{8,10},{9,11},{10,... | collective-permute-start | bytes 393224 | tf_op jit(solution)/shard_map/ppermute | solution.py:335
  49.6 6.6 %collective-permute-start.1 = (f32[256,128]{1,0:T(8,128)S(1)}, f32[256,128]{1,0:T(8,128)S(1)}, u32[]{:S(2)}, u32[]{:S(2)}) collective-permute-start(f32[256,128]{1,0:T(8,128)S(1)} %get-tuple-element.50), channel_id=1, source_target_pairs={{0,1},{1,2},{2,3},{3,0},{4,5},{5,6},{6,7},{7,4},{8,9},{9,10},{10,1... | collective-permute-start | bytes 393224 | tf_op jit(solution)/shard_map/ppermute | solution.py:335
  50.0 6.2 %collective-permute-start.2 = (f32[256,128]{1,0:T(8,128)S(1)}, f32[256,128]{1,0:T(8,128)S(1)}, u32[]{:S(2)}, u32[]{:S(2)}) collective-permute-start(f32[256,128]{1,0:T(8,128)S(1)} %get-tuple-element.51), channel_id=1, source_target_pairs={{0,3},{1,0},{2,1},{3,2},{4,7},{5,4},{6,5},{7,6},{8,11},{9,8},{10,9... | collective-permute-start | bytes 393224 | tf_op jit(solution)/shard_map/ppermute | solution.py:335
  89.0 6.3 %collective-permute-start.3 = (f32[256,128]{1,0:T(8,128)S(1)}, f32[256,128]{1,0:T(8,128)S(1)}, u32[]{:S(2)}, u32[]{:S(2)}) collective-permute-start(f32[256,128]{1,0:T(8,128)S(1)} %get-tuple-element.57), channel_id=1, source_target_pairs={{0,2},{1,3},{2,0},{3,1},{4,6},{5,7},{6,4},{7,5},{8,10},{9,11},{10,... | collective-permute-start | bytes 393224 | tf_op jit(solution)/shard_map/ppermute | solution.py:335
  92.1 5.8 %collective-permute-start.4 = (f32[256,128]{1,0:T(8,128)S(1)}, f32[256,128]{1,0:T(8,128)S(1)}, u32[]{:S(2)}, u32[]{:S(2)}) collective-permute-start(f32[256,128]{1,0:T(8,128)S(1)} %get-tuple-element.59), channel_id=1, source_target_pairs={{0,1},{1,2},{2,3},{3,0},{4,5},{5,6},{6,7},{7,4},{8,9},{9,10},{10,1... | collective-permute-start | bytes 393224 | tf_op jit(solution)/shard_map/ppermute | solution.py:335
  93.6 4.2 %collective-permute-start.5 = (f32[256,128]{1,0:T(8,128)S(1)}, f32[256,128]{1,0:T(8,128)S(1)}, u32[]{:S(2)}, u32[]{:S(2)}) collective-permute-start(f32[256,128]{1,0:T(8,128)S(1)} %get-tuple-element.60), channel_id=1, source_target_pairs={{0,3},{1,0},{2,1},{3,2},{4,7},{5,4},{6,5},{7,6},{8,11},{9,8},{10,9... | collective-permute-start | bytes 393224 | tf_op jit(solution)/shard_map/ppermute | solution.py:335
  131.5 6.3 %collective-permute-start.6 = (f32[256,128]{1,0:T(8,128)S(1)}, f32[256,128]{1,0:T(8,128)S(1)}, u32[]{:S(2)}, u32[]{:S(2)}) collective-permute-start(f32[256,128]{1,0:T(8,128)S(1)} %get-tuple-element.64), channel_id=1, source_target_pairs={{0,2},{1,3},{2,0},{3,1},{4,6},{5,7},{6,4},{7,5},{8,10},{9,11},{10,... | collective-permute-start | bytes 393224 | tf_op jit(solution)/shard_map/ppermute | solution.py:335
  134.2 6.4 %collective-permute-start.7 = (f32[256,128]{1,0:T(8,128)S(1)}, f32[256,128]{1,0:T(8,128)S(1)}, u32[]{:S(2)}, u32[]{:S(2)}) collective-permute-start(f32[256,128]{1,0:T(8,128)S(1)} %get-tuple-element.66), channel_id=1, source_target_pairs={{0,1},{1,2},{2,3},{3,0},{4,5},{5,6},{6,7},{7,4},{8,9},{9,10},{10,1... | collective-permute-start | bytes 393224 | tf_op jit(solution)/shard_map/ppermute | solution.py:335
  135.8 4.8 %collective-permute-start.8 = (f32[256,128]{1,0:T(8,128)S(1)}, f32[256,128]{1,0:T(8,128)S(1)}, u32[]{:S(2)}, u32[]{:S(2)}) collective-permute-start(f32[256,128]{1,0:T(8,128)S(1)} %get-tuple-element.67), channel_id=1, source_target_pairs={{0,3},{1,0},{2,1},{3,2},{4,7},{5,4},{6,5},{7,6},{8,11},{9,8},{10,9... | collective-permute-start | bytes 393224 | tf_op jit(solution)/shard_map/ppermute | solution.py:335
  173.5 6.3 %collective-permute-start.9 = (f32[256,128]{1,0:T(8,128)S(1)}, f32[256,128]{1,0:T(8,128)S(1)}, u32[]{:S(2)}, u32[]{:S(2)}) collective-permute-start(f32[256,128]{1,0:T(8,128)S(1)} %get-tuple-element.69), channel_id=1, source_target_pairs={{0,2},{1,3},{2,0},{3,1},{4,6},{5,7},{6,4},{7,5},{8,10},{9,11},{10,... | collective-permute-start | bytes 393224 | tf_op jit(solution)/shard_map/ppermute | solution.py:335
  176.3 6.4 %collective-permute-start.10 = (f32[256,128]{1,0:T(8,128)S(1)}, f32[256,128]{1,0:T(8,128)S(1)}, u32[]{:S(2)}, u32[]{:S(2)}) collective-permute-start(f32[256,128]{1,0:T(8,128)S(1)} %get-tuple-element.71), channel_id=1, source_target_pairs={{0,1},{1,2},{2,3},{3,0},{4,5},{5,6},{6,7},{7,4},{8,9},{9,10},{10,1... | collective-permute-start | bytes 393224 | tf_op jit(solution)/shard_map/ppermute | solution.py:335
  177.8 4.8 %collective-permute-start.11 = (f32[256,128]{1,0:T(8,128)S(1)}, f32[256,128]{1,0:T(8,128)S(1)}, u32[]{:S(2)}, u32[]{:S(2)}) collective-permute-start(f32[256,128]{1,0:T(8,128)S(1)} %get-tuple-element.72), channel_id=1, source_target_pairs={{0,3},{1,0},{2,1},{3,2},{4,7},{5,4},{6,5},{7,6},{8,11},{9,8},{10,9... | collective-permute-start | bytes 393224 | tf_op jit(solution)/shard_map/ppermute | solution.py:335
  215.7 6.3 %collective-permute-start.12 = (f32[256,128]{1,0:T(8,128)S(1)}, f32[256,128]{1,0:T(8,128)S(1)}, u32[]{:S(2)}, u32[]{:S(2)}) collective-permute-start(f32[256,128]{1,0:T(8,128)S(1)} %get-tuple-element.75), channel_id=1, source_target_pairs={{0,2},{1,3},{2,0},{3,1},{4,6},{5,7},{6,4},{7,5},{8,10},{9,11},{10,... | collective-permute-start | bytes 393224 | tf_op jit(solution)/shard_map/ppermute | solution.py:335
  218.4 6.4 %collective-permute-start.13 = (f32[256,128]{1,0:T(8,128)S(1)}, f32[256,128]{1,0:T(8,128)S(1)}, u32[]{:S(2)}, u32[]{:S(2)}) collective-permute-start(f32[256,128]{1,0:T(8,128)S(1)} %get-tuple-element.77), channel_id=1, source_target_pairs={{0,1},{1,2},{2,3},{3,0},{4,5},{5,6},{6,7},{7,4},{8,9},{9,10},{10,1... | collective-permute-start | bytes 393224 | tf_op jit(solution)/shard_map/ppermute | solution.py:335
  219.9 4.9 %collective-permute-start.14 = (f32[256,128]{1,0:T(8,128)S(1)}, f32[256,128]{1,0:T(8,128)S(1)}, u32[]{:S(2)}, u32[]{:S(2)}) collective-permute-start(f32[256,128]{1,0:T(8,128)S(1)} %get-tuple-element.78), channel_id=1, source_target_pairs={{0,3},{1,0},{2,1},{3,2},{4,7},{5,4},{6,5},{7,6},{8,11},{9,8},{10,9... | collective-permute-start | bytes 393224 | tf_op jit(solution)/shard_map/ppermute | solution.py:335
  259.0 6.0 %collective-permute-start.16 = (f32[256,128]{1,0:T(8,128)S(1)}, f32[256,128]{1,0:T(8,128)S(1)}, u32[]{:S(2)}, u32[]{:S(2)}) collective-permute-start(f32[256,128]{1,0:T(8,128)S(1)} %get-tuple-element.84), channel_id=1, source_target_pairs={{0,1},{1,2},{2,3},{3,0},{4,5},{5,6},{6,7},{7,4},{8,9},{9,10},{10,1... | collective-permute-start | bytes 393224 | tf_op jit(solution)/shard_map/ppermute | solution.py:335
  259.9 5.1 %collective-permute-start.17 = (f32[256,128]{1,0:T(8,128)S(1)}, f32[256,128]{1,0:T(8,128)S(1)}, u32[]{:S(2)}, u32[]{:S(2)}) collective-permute-start(f32[256,128]{1,0:T(8,128)S(1)} %get-tuple-element.85), channel_id=1, source_target_pairs={{0,3},{1,0},{2,1},{3,2},{4,7},{5,4},{6,5},{7,6},{8,11},{9,8},{10,9... | collective-permute-start | bytes 393224 | tf_op jit(solution)/shard_map/ppermute | solution.py:335
  261.7 6.9 %collective-permute-start.15 = (f32[256,128]{1,0:T(8,128)S(1)}, f32[256,128]{1,0:T(8,128)S(1)}, u32[]{:S(2)}, u32[]{:S(2)}) collective-permute-start(f32[256,128]{1,0:T(8,128)S(1)} %get-tuple-element.82), channel_id=1, source_target_pairs={{0,2},{1,3},{2,0},{3,1},{4,6},{5,7},{6,4},{7,5},{8,10},{9,11},{10,... | collective-permute-start | bytes 393224 | tf_op jit(solution)/shard_map/ppermute | solution.py:335

commit v5 on v4

--- a/solution.py
+++ b/solution.py
@@ -68,11 +68,15 @@
     return apply
 
 
-def pack_kernel(rows_ref, out_ref, kept_ref):
+def pack_kernel(rows_ref, out_ref, kept_ref, buffer_ref, arrived):
     row_count = rows_ref.shape[2]
     own = rows_ref.shape[1]
+    copies = [pltpu.make_async_copy(rows_ref.at[:, k], buffer_ref.at[k], arrived.at[k]) for k in range(own)]
+    for copy in copies:
+        copy.start()
     for k in range(own):
-        packed = swap_groups([rows_ref[c, k] for c in range(4)])
+        copies[k].wait()
+        packed = swap_groups([buffer_ref[k, c] for c in range(4)])
         for q in range(4):
             target = pl.ds(q * own * row_count + k, row_count, stride=own)
             out_ref[target, :] = packed[q]
@@ -210,7 +214,7 @@
                 parts_ref[0, k, n * times : (n + 1) * times, m * LANES : (m + 1) * LANES] = high
                 parts_ref[1, k, n * times : (n + 1) * times, m * LANES : (m + 1) * LANES] = low
 
-    products_into(left_ref, parts_ref, out_refs, 0, 1, prepare)
+    products_into(left_ref, parts_ref, out_refs, 0, 2, prepare)
 
 
 def slope_of(parts, state, band_ref):
@@ -284,7 +288,13 @@
     limits = jnp.stack([lax.axis_index("tm"), history_len[0]])
 
     vmem = pltpu.VMEM
-    pack = resident(pack_kernel, [packed_shape] * 2, [vmem], "pack")
+    pack = resident(
+        pack_kernel,
+        [packed_shape] * 2,
+        [pltpu.HBM],
+        "pack",
+        [vmem((own, 4, row_count, time_count), F32), pltpu.SemaphoreType.DMA((own,))],
+    )
     stored = 6 * time_count
     parts_shape = jax.ShapeDtypeStruct((2, own, stored, hist), BF16)
     site = resident(site_kernel, [packed_shape], [vmem] * 2, "site")

time: 270 us -> 271 us (level)
  no operation moved by 1% of the time
where the time goes in v5:
time: 271 us; the launch traced here: 270 us
  blocking collectives  169 us (62%)
  starting transfers between devices  40.1 us (15%)
  waiting for transfers between devices  30.2 us (11%)
  Pallas kernels  25.3 us (9%)
  other arithmetic  3.16 us (1%)
    all_to_all x11, blocking collectives, turned(): return lax.all_to_all(value, 'mom', 0, 0, tiled=True)  169 us
    ppermute x18, starting transfers between devices, exchange(): lax.ppermute(value, 'tm', [(t, (t + place) % tm_size) for t in range(tm_s...  27.1 us
    pallas_call x24, Pallas kernels, apply(): return call(*placed)  25.3 us
    ppermute x18, waiting for transfers between devices, exchange(): lax.ppermute(value, 'tm', [(t, (t + place) % tm_size) for t in range(tm_s...  23.9 us
    all_to_all x1, starting transfers between devices, turned(): return lax.all_to_all(value, 'mom', 0, 0, tiled=True)  13 us
    all_to_all x1, waiting for transfers between devices, turned(): return lax.all_to_all(value, 'mom', 0, 0, tiled=True)  6.35 us
  transfers between devices with their start and end apart: 19, of which 13 were waited for; matrix products, arithmetic and copies ran while one was open for 1% of the time, Pallas kernels for 2%

profile of v5, /device:TPU:1, one launch (start us, length us, event | category | flops | bytes accessed | tf_op | source)
XLA Modules:
  0.0 270.1 jit_solution(121574336383117770)
XLA Ops:
  1.8 13.0 %all-to-all-start = ((f32[64,4,128]{2,1,0:T(4,128)}), f32[64,4,128]{2,1,0:T(4,128)S(1)}, u32[]{:S(2)}, u32[]{:S(2)}) async-start(f32[64,4,128]{2,1,0:T(4,128)} %bitcast), calls=%async_computation | async-start | bytes 262144 | tf_op jit(solution)/shard_map/all_to_all | solution.py:341
  19.6 6.3 %all-to-all-done = f32[64,4,128]{2,1,0:T(4,128)S(1)} async-done(((f32[64,4,128]{2,1,0:T(4,128)}), f32[64,4,128]{2,1,0:T(4,128)S(1)}, u32[]{:S(2)}, u32[]{:S(2)}) %all-to-all-start) | async-done | bytes 131104 | tf_op jit(solution)/shard_map/all_to_all | solution.py:341
  27.2 14.9 %all_to_all.133 = f32[64,4,128]{2,1,0:T(4,128)S(1)} all-to-all(f32[64,4,128]{2,1,0:T(4,128)S(1)} %bitcast.37), channel_id=1, replica_groups=mesh['mom'=64,'tm'=4] {'mom'}, dimensions={0} | all-to-all | bytes 262144 | tf_op jit(solution)/shard_map/all_to_all | solution.py:341
  42.1 4.5 %first_integral.1 = (f32[256,128]{1,0:T(8,128)S(1)}, f32[256,128]{1,0:T(8,128)S(1)}, f32[256,128]{1,0:T(8,128)S(1)}, f32[256,128]{1,0:T(8,128)S(1)}, bf16[2,4,768,512]{3,2,1,0:T(8,128)(2,1)S(1)}) custom-call(s32[2]{0:T(128)S(1)} %pad_add_fusion.limits_ref, f32[256,128]{1,0:T(8,128)S(1)} %bitcast.29, f32[3,2,4,128,512]{4,3,2,1,0:T(8,128)} %stored_ref.1), custom_call_target="tpu_custom_call" | custom-call | tf_op jit(solution)/shard_map/first_integral/pallas_call | solution.py:66
  46.7 3.0 %collective-permute-start = (f32[256,128]{1,0:T(8,128)S(1)}, f32[256,128]{1,0:T(8,128)S(1)}, u32[]{:S(2)}, u32[]{:S(2)}) collective-permute-start(f32[256,128]{1,0:T(8,128)S(1)} %get-tuple-element.49), channel_id=1, source_target_pairs={{0,2},{1,3},{2,0},{3,1},{4,6},{5,7},{6,4},{7,5},{8,10},{9,11},{10,... | collective-permute-start | bytes 393224 | tf_op jit(solution)/shard_map/ppermute | solution.py:345
  50.1 2.3 collective-permute-start.2
  53.0 3.3 %collective-permute-done.1.second_ref = f32[256,128]{1,0:T(8,128)S(1)} collective-permute-done((f32[256,128]{1,0:T(8,128)S(1)}, f32[256,128]{1,0:T(8,128)S(1)}, u32[]{:S(2)}, u32[]{:S(2)}) %collective-permute-start.1) | collective-permute-done | bytes 131104 | tf_op jit(solution)/shard_map/ppermute | solution.py:345
  56.6 15.6 %all_to_all.134 = f32[64,4,128]{2,1,0:T(4,128)S(1)} all-to-all(f32[64,4,128]{2,1,0:T(4,128)S(1)} %bitcast.47), channel_id=1, replica_groups=mesh['mom'=64,'tm'=4] {'mom'}, dimensions={0} | all-to-all | bytes 262144 | tf_op jit(solution)/shard_map/all_to_all | solution.py:341
  73.2 14.9 %all_to_all.135 = f32[64,4,128]{2,1,0:T(4,128)S(1)} all-to-all(f32[64,4,128]{2,1,0:T(4,128)S(1)} %bitcast.38), channel_id=1, replica_groups=mesh['mom'=64,'tm'=4] {'mom'}, dimensions={0} | all-to-all | bytes 262144 | tf_op jit(solution)/shard_map/all_to_all | solution.py:341
  89.2 1.9 collective-permute-start.3
  95.4 2.6 collective-permute-done.4.second_ref
  98.3 16.3 %all_to_all.136 = f32[64,4,128]{2,1,0:T(4,128)S(1)} all-to-all(f32[64,4,128]{2,1,0:T(4,128)S(1)} %bitcast.28), channel_id=1, replica_groups=mesh['mom'=64,'tm'=4] {'mom'}, dimensions={0} | all-to-all | bytes 262144 | tf_op jit(solution)/shard_map/all_to_all | solution.py:341
  115.7 14.9 %all_to_all.137 = f32[64,4,128]{2,1,0:T(4,128)S(1)} all-to-all(f32[64,4,128]{2,1,0:T(4,128)S(1)} %bitcast.39), channel_id=1, replica_groups=mesh['mom'=64,'tm'=4] {'mom'}, dimensions={0} | all-to-all | bytes 262144 | tf_op jit(solution)/shard_map/all_to_all | solution.py:341
  137.9 2.8 %collective-permute-done.7.second_ref = f32[256,128]{1,0:T(8,128)S(1)} collective-permute-done((f32[256,128]{1,0:T(8,128)S(1)}, f32[256,128]{1,0:T(8,128)S(1)}, u32[]{:S(2)}, u32[]{:S(2)}) %collective-permute-start.7) | collective-permute-done | bytes 131104 | tf_op jit(solution)/shard_map/ppermute | solution.py:345
  141.0 15.7 %all_to_all.138 = f32[64,4,128]{2,1,0:T(4,128)S(1)} all-to-all(f32[64,4,128]{2,1,0:T(4,128)S(1)} %bitcast.26), channel_id=1, replica_groups=mesh['mom'=64,'tm'=4] {'mom'}, dimensions={0} | all-to-all | bytes 262144 | tf_op jit(solution)/shard_map/all_to_all | solution.py:341
  157.7 14.9 %all_to_all.139 = f32[64,4,128]{2,1,0:T(4,128)S(1)} all-to-all(f32[64,4,128]{2,1,0:T(4,128)S(1)} %bitcast.40), channel_id=1, replica_groups=mesh['mom'=64,'tm'=4] {'mom'}, dimensions={0} | all-to-all | bytes 262144 | tf_op jit(solution)/shard_map/all_to_all | solution.py:341
  179.9 2.8 %collective-permute-done.10.second_ref = f32[256,128]{1,0:T(8,128)S(1)} collective-permute-done((f32[256,128]{1,0:T(8,128)S(1)}, f32[256,128]{1,0:T(8,128)S(1)}, u32[]{:S(2)}, u32[]{:S(2)}) %collective-permute-start.10) | collective-permute-done | bytes 131104 | tf_op jit(solution)/shard_map/ppermute | solution.py:345
  183.0 16.0 %all_to_all.140 = f32[64,4,128]{2,1,0:T(4,128)S(1)} all-to-all(f32[64,4,128]{2,1,0:T(4,128)S(1)} %bitcast.48), channel_id=1, replica_groups=mesh['mom'=64,'tm'=4] {'mom'}, dimensions={0} | all-to-all | bytes 262144 | tf_op jit(solution)/shard_map/all_to_all | solution.py:341
  200.1 14.9 %all_to_all.141 = f32[64,4,128]{2,1,0:T(4,128)S(1)} all-to-all(f32[64,4,128]{2,1,0:T(4,128)S(1)} %bitcast.41), channel_id=1, replica_groups=mesh['mom'=64,'tm'=4] {'mom'}, dimensions={0} | all-to-all | bytes 262144 | tf_op jit(solution)/shard_map/all_to_all | solution.py:341
  222.3 2.8 %collective-permute-done.13.second_ref = f32[256,128]{1,0:T(8,128)S(1)} collective-permute-done((f32[256,128]{1,0:T(8,128)S(1)}, f32[256,128]{1,0:T(8,128)S(1)}, u32[]{:S(2)}, u32[]{:S(2)}) %collective-permute-start.13) | collective-permute-done | bytes 131104 | tf_op jit(solution)/shard_map/ppermute | solution.py:345
  225.4 15.7 %all_to_all.142 = f32[64,4,128]{2,1,0:T(4,128)S(1)} all-to-all(f32[64,4,128]{2,1,0:T(4,128)S(1)} %bitcast.27), channel_id=1, replica_groups=mesh['mom'=64,'tm'=4] {'mom'}, dimensions={0} | all-to-all | bytes 262144 | tf_op jit(solution)/shard_map/all_to_all | solution.py:341
  242.1 14.9 %all_to_all.143 = f32[64,4,128]{2,1,0:T(4,128)S(1)} all-to-all(f32[64,4,128]{2,1,0:T(4,128)S(1)} %bitcast.36), channel_id=1, replica_groups=mesh['mom'=64,'tm'=4] {'mom'}, dimensions={0} | all-to-all | bytes 262144 | tf_op jit(solution)/shard_map/all_to_all | solution.py:341
  263.0 2.2 collective-permute-done.16.second_ref
  265.2 3.8 %collective-permute-done.15.first_ref = f32[256,128]{1,0:T(8,128)S(1)} collective-permute-done((f32[256,128]{1,0:T(8,128)S(1)}, f32[256,128]{1,0:T(8,128)S(1)}, u32[]{:S(2)}, u32[]{:S(2)}) %collective-permute-start.15) | collective-permute-done | bytes 131104 | tf_op jit(solution)/shard_map/ppermute | solution.py:345
  (65 shorter events, 48.4 us)
Async XLA Ops:
  1.8 24.1 %all-to-all-start = ((f32[64,4,128]{2,1,0:T(4,128)}), f32[64,4,128]{2,1,0:T(4,128)S(1)}, u32[]{:S(2)}, u32[]{:S(2)}) async-start(f32[64,4,128]{2,1,0:T(4,128)} %bitcast), calls=%async_computation | async-start | bytes 262144 | tf_op jit(solution)/shard_map/all_to_all | solution.py:341
  46.7 6.3 %collective-permute-start = (f32[256,128]{1,0:T(8,128)S(1)}, f32[256,128]{1,0:T(8,128)S(1)}, u32[]{:S(2)}, u32[]{:S(2)}) collective-permute-start(f32[256,128]{1,0:T(8,128)S(1)} %get-tuple-element.49), channel_id=1, source_target_pairs={{0,2},{1,3},{2,0},{3,1},{4,6},{5,7},{6,4},{7,5},{8,10},{9,11},{10,... | collective-permute-start | bytes 393224 | tf_op jit(solution)/shard_map/ppermute | solution.py:345
  49.7 6.6 %collective-permute-start.1 = (f32[256,128]{1,0:T(8,128)S(1)}, f32[256,128]{1,0:T(8,128)S(1)}, u32[]{:S(2)}, u32[]{:S(2)}) collective-permute-start(f32[256,128]{1,0:T(8,128)S(1)} %get-tuple-element.50), channel_id=1, source_target_pairs={{0,1},{1,2},{2,3},{3,0},{4,5},{5,6},{6,7},{7,4},{8,9},{9,10},{10,1... | collective-permute-start | bytes 393224 | tf_op jit(solution)/shard_map/ppermute | solution.py:345
  50.1 6.2 %collective-permute-start.2 = (f32[256,128]{1,0:T(8,128)S(1)}, f32[256,128]{1,0:T(8,128)S(1)}, u32[]{:S(2)}, u32[]{:S(2)}) collective-permute-start(f32[256,128]{1,0:T(8,128)S(1)} %get-tuple-element.51), channel_id=1, source_target_pairs={{0,3},{1,0},{2,1},{3,2},{4,7},{5,4},{6,5},{7,6},{8,11},{9,8},{10,9... | collective-permute-start | bytes 393224 | tf_op jit(solution)/shard_map/ppermute | solution.py:345
  89.2 6.3 %collective-permute-start.3 = (f32[256,128]{1,0:T(8,128)S(1)}, f32[256,128]{1,0:T(8,128)S(1)}, u32[]{:S(2)}, u32[]{:S(2)}) collective-permute-start(f32[256,128]{1,0:T(8,128)S(1)} %get-tuple-element.57), channel_id=1, source_target_pairs={{0,2},{1,3},{2,0},{3,1},{4,6},{5,7},{6,4},{7,5},{8,10},{9,11},{10,... | collective-permute-start | bytes 393224 | tf_op jit(solution)/shard_map/ppermute | solution.py:345
  92.2 5.8 %collective-permute-start.4 = (f32[256,128]{1,0:T(8,128)S(1)}, f32[256,128]{1,0:T(8,128)S(1)}, u32[]{:S(2)}, u32[]{:S(2)}) collective-permute-start(f32[256,128]{1,0:T(8,128)S(1)} %get-tuple-element.59), channel_id=1, source_target_pairs={{0,1},{1,2},{2,3},{3,0},{4,5},{5,6},{6,7},{7,4},{8,9},{9,10},{10,1... | collective-permute-start | bytes 393224 | tf_op jit(solution)/shard_map/ppermute | solution.py:345
  93.8 4.2 %collective-permute-start.5 = (f32[256,128]{1,0:T(8,128)S(1)}, f32[256,128]{1,0:T(8,128)S(1)}, u32[]{:S(2)}, u32[]{:S(2)}) collective-permute-start(f32[256,128]{1,0:T(8,128)S(1)} %get-tuple-element.60), channel_id=1, source_target_pairs={{0,3},{1,0},{2,1},{3,2},{4,7},{5,4},{6,5},{7,6},{8,11},{9,8},{10,9... | collective-permute-start | bytes 393224 | tf_op jit(solution)/shard_map/ppermute | solution.py:345
  131.6 6.3 %collective-permute-start.6 = (f32[256,128]{1,0:T(8,128)S(1)}, f32[256,128]{1,0:T(8,128)S(1)}, u32[]{:S(2)}, u32[]{:S(2)}) collective-permute-start(f32[256,128]{1,0:T(8,128)S(1)} %get-tuple-element.64), channel_id=1, source_target_pairs={{0,2},{1,3},{2,0},{3,1},{4,6},{5,7},{6,4},{7,5},{8,10},{9,11},{10,... | collective-permute-start | bytes 393224 | tf_op jit(solution)/shard_map/ppermute | solution.py:345
  134.3 6.4 %collective-permute-start.7 = (f32[256,128]{1,0:T(8,128)S(1)}, f32[256,128]{1,0:T(8,128)S(1)}, u32[]{:S(2)}, u32[]{:S(2)}) collective-permute-start(f32[256,128]{1,0:T(8,128)S(1)} %get-tuple-element.66), channel_id=1, source_target_pairs={{0,1},{1,2},{2,3},{3,0},{4,5},{5,6},{6,7},{7,4},{8,9},{9,10},{10,1... | collective-permute-start | bytes 393224 | tf_op jit(solution)/shard_map/ppermute | solution.py:345
  135.9 4.8 %collective-permute-start.8 = (f32[256,128]{1,0:T(8,128)S(1)}, f32[256,128]{1,0:T(8,128)S(1)}, u32[]{:S(2)}, u32[]{:S(2)}) collective-permute-start(f32[256,128]{1,0:T(8,128)S(1)} %get-tuple-element.67), channel_id=1, source_target_pairs={{0,3},{1,0},{2,1},{3,2},{4,7},{5,4},{6,5},{7,6},{8,11},{9,8},{10,9... | collective-permute-start | bytes 393224 | tf_op jit(solution)/shard_map/ppermute | solution.py:345
  173.6 6.3 %collective-permute-start.9 = (f32[256,128]{1,0:T(8,128)S(1)}, f32[256,128]{1,0:T(8,128)S(1)}, u32[]{:S(2)}, u32[]{:S(2)}) collective-permute-start(f32[256,128]{1,0:T(8,128)S(1)} %get-tuple-element.69), channel_id=1, source_target_pairs={{0,2},{1,3},{2,0},{3,1},{4,6},{5,7},{6,4},{7,5},{8,10},{9,11},{10,... | collective-permute-start | bytes 393224 | tf_op jit(solution)/shard_map/ppermute | solution.py:345
  176.4 6.4 %collective-permute-start.10 = (f32[256,128]{1,0:T(8,128)S(1)}, f32[256,128]{1,0:T(8,128)S(1)}, u32[]{:S(2)}, u32[]{:S(2)}) collective-permute-start(f32[256,128]{1,0:T(8,128)S(1)} %get-tuple-element.71), channel_id=1, source_target_pairs={{0,1},{1,2},{2,3},{3,0},{4,5},{5,6},{6,7},{7,4},{8,9},{9,10},{10,1... | collective-permute-start | bytes 393224 | tf_op jit(solution)/shard_map/ppermute | solution.py:345
  177.9 4.8 %collective-permute-start.11 = (f32[256,128]{1,0:T(8,128)S(1)}, f32[256,128]{1,0:T(8,128)S(1)}, u32[]{:S(2)}, u32[]{:S(2)}) collective-permute-start(f32[256,128]{1,0:T(8,128)S(1)} %get-tuple-element.72), channel_id=1, source_target_pairs={{0,3},{1,0},{2,1},{3,2},{4,7},{5,4},{6,5},{7,6},{8,11},{9,8},{10,9... | collective-permute-start | bytes 393224 | tf_op jit(solution)/shard_map/ppermute | solution.py:345
  216.0 6.3 %collective-permute-start.12 = (f32[256,128]{1,0:T(8,128)S(1)}, f32[256,128]{1,0:T(8,128)S(1)}, u32[]{:S(2)}, u32[]{:S(2)}) collective-permute-start(f32[256,128]{1,0:T(8,128)S(1)} %get-tuple-element.75), channel_id=1, source_target_pairs={{0,2},{1,3},{2,0},{3,1},{4,6},{5,7},{6,4},{7,5},{8,10},{9,11},{10,... | collective-permute-start | bytes 393224 | tf_op jit(solution)/shard_map/ppermute | solution.py:345
  218.8 6.4 %collective-permute-start.13 = (f32[256,128]{1,0:T(8,128)S(1)}, f32[256,128]{1,0:T(8,128)S(1)}, u32[]{:S(2)}, u32[]{:S(2)}) collective-permute-start(f32[256,128]{1,0:T(8,128)S(1)} %get-tuple-element.77), channel_id=1, source_target_pairs={{0,1},{1,2},{2,3},{3,0},{4,5},{5,6},{6,7},{7,4},{8,9},{9,10},{10,1... | collective-permute-start | bytes 393224 | tf_op jit(solution)/shard_map/ppermute | solution.py:345
  220.3 4.8 %collective-permute-start.14 = (f32[256,128]{1,0:T(8,128)S(1)}, f32[256,128]{1,0:T(8,128)S(1)}, u32[]{:S(2)}, u32[]{:S(2)}) collective-permute-start(f32[256,128]{1,0:T(8,128)S(1)} %get-tuple-element.78), channel_id=1, source_target_pairs={{0,3},{1,0},{2,1},{3,2},{4,7},{5,4},{6,5},{7,6},{8,11},{9,8},{10,9... | collective-permute-start | bytes 393224 | tf_op jit(solution)/shard_map/ppermute | solution.py:345
  259.2 6.0 %collective-permute-start.16 = (f32[256,128]{1,0:T(8,128)S(1)}, f32[256,128]{1,0:T(8,128)S(1)}, u32[]{:S(2)}, u32[]{:S(2)}) collective-permute-start(f32[256,128]{1,0:T(8,128)S(1)} %get-tuple-element.84), channel_id=1, source_target_pairs={{0,1},{1,2},{2,3},{3,0},{4,5},{5,6},{6,7},{7,4},{8,9},{9,10},{10,1... | collective-permute-start | bytes 393224 | tf_op jit(solution)/shard_map/ppermute | solution.py:345
  260.1 5.1 %collective-permute-start.17 = (f32[256,128]{1,0:T(8,128)S(1)}, f32[256,128]{1,0:T(8,128)S(1)}, u32[]{:S(2)}, u32[]{:S(2)}) collective-permute-start(f32[256,128]{1,0:T(8,128)S(1)} %get-tuple-element.85), channel_id=1, source_target_pairs={{0,3},{1,0},{2,1},{3,2},{4,7},{5,4},{6,5},{7,6},{8,11},{9,8},{10,9... | collective-permute-start | bytes 393224 | tf_op jit(solution)/shard_map/ppermute | solution.py:345
  262.0 7.0 %collective-permute-start.15 = (f32[256,128]{1,0:T(8,128)S(1)}, f32[256,128]{1,0:T(8,128)S(1)}, u32[]{:S(2)}, u32[]{:S(2)}) collective-permute-start(f32[256,128]{1,0:T(8,128)S(1)} %get-tuple-element.82), channel_id=1, source_target_pairs={{0,2},{1,3},{2,0},{3,1},{4,6},{5,7},{6,4},{7,5},{8,10},{9,11},{10,... | collective-permute-start | bytes 393224 | tf_op jit(solution)/shard_map/ppermute | solution.py:345
